TPU v7x, 32 devices: a whole 2x2x4 slice. The times are simulated.
32 devices in a mesh: stream: 4 (over y, core), trans: 8 (over z, x).
Axes of the slice: x: 2, y: 2, z: 4, core: 2. Of those that a mesh axis runs over, the one named last changes fastest.
Arguments:
- populations: float32 [19, 8, 64, 128], P(None, 'stream', 'trans'), may hold values from 0.01 to 0.2
- solid: int32 [8, 64, 128], P('stream', 'trans'), may hold values 0 or 1
- support: int32 [4096], P(('stream', 'trans')), may hold values from 0 to 8062, as said below
- fractions: float32 [3, 4096], P(None, ('stream', 'trans')), may hold values from 0 to 1
- target: float32 [3, 4096], P(None, ('stream', 'trans')), may hold values from -0.1 to 0.1
- area: float32 [4096], P(('stream', 'trans')), may hold values from 1 to 4
Outputs:
- new_populations: float32 [19, 8, 64, 128], P(None, 'stream', 'trans')
- marker_force: float32 [3, 4096], P(None, ('stream', 'trans'))
Inputs may be any that keep to these rules, and one draw needn't show every extreme that they name: support[m] = (a * 64 + b) * 128 + e with a = 0 counted inside marker m's streamwise slab m // (128 * 8) (each cube spans the slab's two planes), 0 <= b <= 64 - 2 over the whole first transverse dimension and 0 <= e <= 126.
All inputs are finite; a program needn't handle non-finite values. No bound on the sum of `solid` on one device may be relied on, other than what follows from the above.
Results may differ from a plain program's by a relative error of at most 0.0003.
Values sent between devices are 32-bit elements; how exact they have to be, the bound alone decides.
No kernel may reach another device: no remote copies, remote signals or barrier semaphores. Data moves between devices by JAX's collectives and lax.ppermute only.
A program may use at most 64 MiB of HBM per device.

v0:
```python
import math

import jax
import jax.numpy as jnp
from jax import lax
from jax.sharding import PartitionSpec as P

STEPS = 2


velocity_table = (
    (0, 0, 0),
    (1, 0, 0),
    (-1, 0, 0),
    (0, 1, 0),
    (0, -1, 0),
    (0, 0, 1),
    (0, 0, -1),
    (1, 1, 0),
    (-1, -1, 0),
    (1, -1, 0),
    (-1, 1, 0),
    (1, 0, 1),
    (-1, 0, -1),
    (1, 0, -1),
    (-1, 0, 1),
    (0, 1, 1),
    (0, -1, -1),
    (0, 1, -1),
    (0, -1, 1),
)
weight_table = (1.0 / 3.0,) + (1.0 / 18.0,) * 6 + (1.0 / 36.0,) * 12
opposite = (0, 2, 1, 4, 3, 6, 5, 8, 7, 10, 9, 12, 11, 14, 13, 16, 15, 18, 17)
relax_base = 0.8
smagorinsky = 0.17


def extended(block, sides, width):
    for axis, dim in sides:
        count = lax.axis_size(axis)
        forward = [(i, i + 1) for i in range(count - 1)]
        forward.append((count - 1, 0))
        backward = [(target, source) for source, target in forward]
        low = lax.ppermute(
            lax.slice_in_dim(block, block.shape[dim] - width, None, axis=dim), axis, forward
        )
        high = lax.ppermute(lax.slice_in_dim(block, 0, width, axis=dim), axis, backward)
        block = jnp.concatenate([low, block, high], axis=dim)
    return block


def signed_sum(factors, values):
    running = None
    for factor, value in zip(factors, values):
        if factor != 0:
            signed_term = value if factor > 0 else -value
            running = signed_term if running is None else running + signed_term
    return 0.0 if running is None else running


def moments(fields):
    density = fields[0]
    for member in range(1, 19):
        density = density + fields[member]
    momenta = []
    for dimension in range(3):
        momenta.append(
            signed_sum(
                [velocity_table[member][dimension] for member in range(19)],
                [fields[member] for member in range(19)],
            )
        )
    return (density, momenta)


def collide(fields, density, momenta, forcing, solid):
    velocity = [(momenta[dimension] + 0.5 * forcing[dimension]) / density for dimension in range(3)]
    square = velocity[0] * velocity[0] + velocity[1] * velocity[1] + velocity[2] * velocity[2]
    force_along = velocity[0] * forcing[0] + velocity[1] * forcing[1] + velocity[2] * forcing[2]
    projections = []
    nonequil = []
    for member in range(19):
        projected = signed_sum(velocity_table[member], velocity)
        equilibrium = (
            weight_table[member]
            * density
            * (1.0 + 3.0 * projected + 4.5 * projected * projected - 1.5 * square)
        )
        projections.append(projected)
        nonequil.append(fields[member] - equilibrium)
    magnitude_square = 0.0
    for first, second in ((0, 0), (1, 1), (2, 2), (0, 1), (0, 2), (1, 2)):
        component = signed_sum(
            [
                velocity_table[member][first] * velocity_table[member][second]
                for member in range(19)
            ],
            nonequil,
        )
        factor = 1.0 if first == second else 2.0
        magnitude_square = magnitude_square + factor * component * component
    magnitude = jnp.sqrt(magnitude_square)
    relaxation = 0.5 * (
        relax_base
        + jnp.sqrt(
            relax_base * relax_base
            + 18.0 * math.sqrt(2.0) * smagorinsky * smagorinsky * magnitude / density
        )
    )
    force_share = 1.0 - 0.5 / relaxation
    outputs = []
    for member in range(19):
        along_force = signed_sum(velocity_table[member], forcing)
        source = (
            force_share
            * weight_table[member]
            * (3.0 * (along_force - force_along) + 9.0 * projections[member] * along_force)
        )
        collided = fields[member] - nonequil[member] / relaxation + source
        outputs.append(jnp.where(solid == 1, fields[opposite[member]], collided))
    return jnp.stack(outputs)


def linear_share(fraction, offset):
    return fraction if offset else 1.0 - fraction


def propagate(collided):
    plane_count = collided.shape[1]
    row_count = collided.shape[2]
    moved = [collided[member] for member in range(19)]
    along_x = [member for member in range(19) if velocity_table[member][0] != 0]
    padded_x = extended(jnp.stack([moved[member] for member in along_x]), (("stream", 1),), 1)
    for position, member in enumerate(along_x):
        start_x = 1 - velocity_table[member][0]
        moved[member] = padded_x[position, start_x : start_x + plane_count]
    along_y = [member for member in range(19) if velocity_table[member][1] != 0]
    padded_y = extended(jnp.stack([moved[member] for member in along_y]), (("trans", 2),), 1)
    for position, member in enumerate(along_y):
        start_y = 1 - velocity_table[member][1]
        moved[member] = padded_y[position, :, start_y : start_y + row_count]
    rolled = []
    for member in range(19):
        depth_shift = velocity_table[member][2]
        rolled.append(
            jnp.roll(moved[member], depth_shift, axis=-1) if depth_shift != 0 else moved[member]
        )
    return jnp.stack(rolled)


def weight_tables(
    block_support, block_fraction, plane_count, row_count, depth_count, total_rows, own_rank
):
    depth_index = block_support % depth_count
    remainder = block_support // depth_count
    column = remainder % total_rows
    plane_index = remainder // total_rows
    pair_iota = jnp.arange(plane_count * row_count, dtype=jnp.int32)
    depth_iota = jnp.arange(depth_count, dtype=jnp.int32)
    pair_weight = jnp.zeros((block_support.shape[0], plane_count * row_count), jnp.float32)
    for shift_x in (0, 1):
        for shift_y in (0, 1):
            local_row = column + shift_y - own_rank * row_count
            valid = (local_row >= 0) & (local_row < row_count)
            pair_index = jnp.where(valid, (plane_index + shift_x) * row_count + local_row, -1)
            share = linear_share(block_fraction[0], shift_x) * linear_share(
                block_fraction[1], shift_y
            )
            pair_weight = pair_weight + jnp.where(
                pair_iota[None, :] == pair_index[:, None], share[:, None], 0.0
            )
    depth_weight = jnp.where(
        depth_iota[None, :] == depth_index[:, None], (1.0 - block_fraction[2])[:, None], 0.0
    ) + jnp.where(depth_iota[None, :] == depth_index[:, None] + 1, block_fraction[2][:, None], 0.0)
    return (pair_weight, depth_weight)


def per_device(populations, solid, support, fractions, target, area):
    plane_count = populations.shape[1]
    row_count = populations.shape[2]
    depth_count = populations.shape[3]
    own_markers = support.shape[0]
    groups = lax.axis_size("trans")
    own_rank = lax.axis_index("trans")
    total_rows = row_count * groups
    group_support, group_fraction, group_target, group_area = (
        lax.all_gather(support, "trans", axis=0, tiled=True),
        lax.all_gather(fractions, "trans", axis=1, tiled=True),
        lax.all_gather(target, "trans", axis=1, tiled=True),
        lax.all_gather(area, "trans", axis=0, tiled=True),
    )
    group_count = group_support.shape[0]
    block_size = math.gcd(group_count, 256)
    block_count = group_count // block_size
    support_blocks = group_support.reshape(block_count, block_size)
    fraction_blocks = jnp.moveaxis(group_fraction.reshape(3, block_count, block_size), 1, 0)
    fields = populations
    own_force = jnp.zeros((3, own_markers), jnp.float32)
    for repeat in range(STEPS):
        density, momenta = moments(fields)
        velocity_field = jnp.stack(
            [momenta[dimension] / density for dimension in range(3)]
        ).reshape(3, plane_count * row_count, depth_count)

        def interpolate(block):
            pair_weight, depth_weight = weight_tables(
                block[0], block[1], plane_count, row_count, depth_count, total_rows, own_rank
            )
            along_pairs = jnp.einsum(
                "mp,cpd->cmd", pair_weight, velocity_field, precision=lax.Precision.HIGHEST
            )
            return jnp.sum(along_pairs * depth_weight[None], axis=2)

        block_velocity = lax.map(interpolate, (support_blocks, fraction_blocks))
        partial_velocity = jnp.moveaxis(block_velocity, 0, 1).reshape(3, group_count)
        velocity = lax.psum(partial_velocity, "trans")
        group_force = group_area * (group_target - velocity)
        own_force = lax.dynamic_slice_in_dim(group_force, own_rank * own_markers, own_markers, 1)
        force_blocks = jnp.moveaxis(group_force.reshape(3, block_count, block_size), 1, 0)

        def spread(total, block):
            pair_weight, depth_weight = weight_tables(
                block[0], block[1], plane_count, row_count, depth_count, total_rows, own_rank
            )
            weighted = block[2][:, :, None] * depth_weight[None]
            added = jnp.einsum(
                "mp,cmd->cpd", pair_weight, weighted, precision=lax.Precision.HIGHEST
            )
            return (total + added, None)

        forcing, unused = lax.scan(
            spread,
            jnp.zeros((3, plane_count * row_count, depth_count), jnp.float32),
            (support_blocks, fraction_blocks, force_blocks),
        )
        forcing = forcing.reshape(3, plane_count, row_count, depth_count)
        collided = collide(fields, density, momenta, forcing, solid)
        fields = propagate(collided)
    return (fields, own_force)


def solution(mesh):
    placed = (
        P(None, "stream", "trans", None),
        P("stream", "trans", None),
        P(("stream", "trans")),
        P(None, ("stream", "trans")),
        P(None, ("stream", "trans")),
        P(("stream", "trans")),
    )
    return jax.shard_map(
        per_device,
        mesh=mesh,
        in_specs=placed,
        out_specs=(P(None, "stream", "trans", None), P(None, ("stream", "trans"))),
        check_vma=False,
    )
```

profile of v0, /device:TPU:0, one launch (start us, length us, event | category | flops | bytes accessed | tf_op | source)
XLA Modules:
  0.0 197.4 jit_solution(17173146682361755467)
XLA Ops:
  0.6 0.9 divide_bitcast_fusion.5
  1.8 0.6 copy-done.4
  2.4 22.3 %all-gather.1 = s32[8,1,128]{2,1,0:T(1,128)S(1)} all-gather(s32[1,1,128]{2,1,0:T(1,128)S(1)} %bitcast.1152), channel_id=1, replica_groups=mesh['stream'=4,'trans'=8] {'trans'}, dimensions={0}, use_global_device_ids=true | all-gather | bytes 4608 | tf_op jit(solution)/shard_map/all_gather | solution.py:187
  25.2 0.6 reduce.5
  25.8 0.6 copy-done.5
  26.5 16.4 %all-gather = f32[8,1,128]{2,1,0:T(1,128)S(1)} all-gather(f32[1,1,128]{2,1,0:T(1,128)S(1)} %bitcast.1153), channel_id=1, replica_groups=mesh['stream'=4,'trans'=8] {'trans'}, dimensions={0}, use_global_device_ids=true | all-gather | bytes 4608 | tf_op jit(solution)/shard_map/all_gather | solution.py:190
  42.9 26.2 %all_gather.13 = f32[3,1024]{1,0:T(4,128)S(1)} all-gather(f32[3,128]{1,0:T(4,128)S(1)} %copy-done.2), channel_id=1, replica_groups=mesh['stream'=4,'trans'=8] {'trans'}, dimensions={1}, use_global_device_ids=true | all-gather | bytes 13824 | tf_op jit(solution)/shard_map/all_gather | solution.py:189
  69.1 26.1 %all_gather.15 = f32[3,1024]{1,0:T(4,128)S(1)} all-gather(f32[3,128]{1,0:T(4,128)S(1)} %copy-done.3), channel_id=1, replica_groups=mesh['stream'=4,'trans'=8] {'trans'}, dimensions={1}, use_global_device_ids=true | all-gather | bytes 13824 | tf_op jit(solution)/shard_map/all_gather | solution.py:188
  95.2 2.9 %while.54 = (s32[]{:T(128)}, f32[4,3,256]{2,1,0:T(4,128)S(1)}, s32[4,256]{1,0:T(4,128)S(1)}, s32[]{:T(128)}, f32[4,3,256]{2,1,0:T(4,128)S(1)}, /*index=5*/f32[3,...) while((s32[]{:T(128)}, f32[4,3,256]{2,1,0:T(4,128)S(1)}, s32[4,256]{1,0:T(4,128)S(1)}, s32[]{:T(128)}, ...), condition=%wide.region_2.3_spmd, body=%wide.region_0.2_spmd.sunk | while | flops 19297284 | bytes 340129 | solution.py:214
  95.4 0.5 fusion.363
  96.1 0.5 fusion.363
  96.9 0.5 fusion.363
  97.6 0.5 fusion.363
  98.2 33.0 %psum.14 = f32[3,1024]{1,0:T(4,128)S(1)} all-reduce(f32[3,1024]{1,0:T(4,128)S(1)} %bitcast.1149), channel_id=1, replica_groups=mesh['stream'=4,'trans'=8] {'trans'}, use_global_device_ids=true, to_apply=%region_3.4 | all-reduce | flops 3072 | bytes 24576 | tf_op jit(solution)/shard_map/psum | solution.py:216
  131.2 3.1 %while.56 = (s32[]{:T(128)}, f32[3,16,128]{2,1,0:T(8,128)S(1)}, f32[4,3,256]{2,1,0:T(4,128)S(1)}, s32[4,256]{1,0:T(4,128)S(1)}, f32[4,3,256]{2,1,0:T(4,128)S(1)}...) while((s32[]{:T(128)}, f32[3,16,128]{2,1,0:T(8,128)S(1)}, f32[4,3,256]{2,1,0:T(4,128)S(1)}, ...), condition=%wide.region_5.6_spmd.clone, body=%wide.region_4.5_spmd.clone.sunk | while | flops 19212036 | bytes 362667 | solution.py:231
  134.8 1.7 collective-permute-start.1
  136.5 1.7 collective-permute-done
  138.4 2.0 %collective-permute-start.2 = (f32[10,2,1,128]{3,2,1,0:T(1,128)S(1)}, f32[10,2,1,128]{3,2,1,0:T(1,128)S(1)}, u32[]{:S(2)}, u32[]{:S(2)}) collective-permute-start(f32[10,2,1,128]{3,2,1,0:T(1,128)S(1)} %get-tuple-element.707), channel_id=1, source_target_pairs={{0,1},{1,2},{2,3},{3,4},{4,5},{5,6},{6,7},{7,0},{8,9},{9,10},{10,1... | collective-permute-start | bytes 30728 | tf_op jit(solution)/shard_map/ppermute | solution.py:44
  140.9 1.2 collective-permute-done.3
  142.1 2.8 %collective-permute-done.2 = f32[10,2,1,128]{3,2,1,0:T(1,128)S(1)} collective-permute-done((f32[10,2,1,128]{3,2,1,0:T(1,128)S(1)}, f32[10,2,1,128]{3,2,1,0:T(1,128)S(1)}, u32[]{:S(2)}, u32[]{:S(2)}) %collective-permute-start.2) | collective-permute-done | bytes 10272 | tf_op jit(solution)/shard_map/ppermute | solution.py:44
  145.3 2.9 %while.55 = (s32[]{:T(128)}, f32[4,3,256]{2,1,0:T(4,128)S(1)}, s32[4,256]{1,0:T(4,128)S(1)}, s32[]{:T(128)}, f32[4,3,256]{2,1,0:T(4,128)S(1)}, /*index=5*/f32[3,...) while((s32[]{:T(128)}, f32[4,3,256]{2,1,0:T(4,128)S(1)}, s32[4,256]{1,0:T(4,128)S(1)}, s32[]{:T(128)}, ...), condition=%wide.region_8.9_spmd, body=%wide.region_6.8_spmd.sunk | while | flops 19297284 | bytes 340129 | solution.py:214
  145.5 0.5 fusion.366
  146.9 0.5 fusion.366
  148.2 33.0 %psum.15 = f32[3,1024]{1,0:T(4,128)S(1)} all-reduce(f32[3,1024]{1,0:T(4,128)S(1)} %bitcast.1148), channel_id=1, replica_groups=mesh['stream'=4,'trans'=8] {'trans'}, use_global_device_ids=true, to_apply=%region_9.10 | all-reduce | flops 3072 | bytes 24576 | tf_op jit(solution)/shard_map/psum | solution.py:216
  181.2 3.1 %while.57 = (s32[]{:T(128)}, f32[3,16,128]{2,1,0:T(8,128)S(1)}, f32[4,3,256]{2,1,0:T(4,128)S(1)}, s32[4,256]{1,0:T(4,128)S(1)}, f32[4,3,256]{2,1,0:T(4,128)S(1)}...) while((s32[]{:T(128)}, f32[3,16,128]{2,1,0:T(8,128)S(1)}, f32[4,3,256]{2,1,0:T(4,128)S(1)}, ...), condition=%wide.region_11.12_spmd.clone, body=%wide.region_10.11_spmd.clone.sunk | while | flops 19212036 | bytes 362667 | solution.py:231
  184.8 1.8 collective-permute-start.5
  186.6 1.6 collective-permute-done.4
  188.5 0.6 constant_dynamic-slice_fusion.16
  189.5 4.7 %collective-permute-start.7 = (f32[10,2,1,128]{3,2,1,0:T(1,128)S(1)}, f32[10,2,1,128]{3,2,1,0:T(1,128)S(1)}, u32[]{:S(2)}, u32[]{:S(2)}) collective-permute-start(f32[10,2,1,128]{3,2,1,0:T(1,128)S(1)} %get-tuple-element.700), channel_id=1, source_target_pairs={{1,0},{2,1},{3,2},{4,3},{5,4},{6,5},{7,6},{0,7},{9,8},{10,9},{11,1... | collective-permute-start | bytes 30728 | tf_op jit(solution)/shard_map/ppermute | solution.py:47
  194.2 0.6 collective-permute-done.6
  194.9 0.8 collective-permute-done.7
  196.7 0.7 copy-done.6
  (265 shorter events, 11.8 us)
Async XLA Ops:
  0.6 1.1 copy-start
  1.8 0.7 copy-start.4
  25.8 0.7 copy-start.5
  26.5 16.4 %copy-start.2 = (f32[3,128]{1,0:T(4,128)S(1)}, f32[3,128]{1,0:T(4,128)}, u32[]{:S(2)}) copy-start(f32[3,128]{1,0:T(4,128)} %param.18) | copy-start | bytes 4612
  42.9 26.2 %copy-start.3 = (f32[3,128]{1,0:T(4,128)S(1)}, f32[3,128]{1,0:T(4,128)}, u32[]{:S(2)}) copy-start(f32[3,128]{1,0:T(4,128)} %param.17) | copy-start | bytes 4612
  131.1 3.1 %copy-start.1 = (s32[2,8,128]{2,1,0:T(8,128)S(1)}, s32[2,8,128]{2,1,0:T(8,128)}, u32[]{:S(2)}) copy-start(s32[2,8,128]{2,1,0:T(8,128)} %param.15) | copy-start | bytes 24580
  134.7 3.5 %collective-permute-start = (f32[10,1,8,128]{3,2,1,0:T(8,128)S(1)}, f32[10,1,8,128]{3,2,1,0:T(8,128)S(1)}, u32[]{:S(2)}, u32[]{:S(2)}) collective-permute-start(f32[10,1,8,128]{3,2,1,0:T(8,128)S(1)} %get-tuple-element.709), channel_id=1, source_target_pairs={{0,8},{8,16},{16,24},{24,0},{1,9},{9,17},{17,25},{25,1},{2,10},{10... | collective-permute-start | bytes 122888 | tf_op jit(solution)/shard_map/ppermute | solution.py:44
  134.8 3.4 %collective-permute-start.1 = (f32[10,1,8,128]{3,2,1,0:T(8,128)S(1)}, f32[10,1,8,128]{3,2,1,0:T(8,128)S(1)}, u32[]{:S(2)}, u32[]{:S(2)}) collective-permute-start(f32[10,1,8,128]{3,2,1,0:T(8,128)S(1)} %get-tuple-element.708), channel_id=1, source_target_pairs={{8,0},{16,8},{24,16},{0,24},{9,1},{17,9},{25,17},{1,25},{10,2},{18... | collective-permute-start | bytes 122888 | tf_op jit(solution)/shard_map/ppermute | solution.py:47
  138.4 3.7 %collective-permute-start.3 = (f32[10,2,1,128]{3,2,1,0:T(1,128)S(1)}, f32[10,2,1,128]{3,2,1,0:T(1,128)S(1)}, u32[]{:S(2)}, u32[]{:S(2)}) collective-permute-start(f32[10,2,1,128]{3,2,1,0:T(1,128)S(1)} %get-tuple-element.706), channel_id=1, source_target_pairs={{1,0},{2,1},{3,2},{4,3},{5,4},{6,5},{7,6},{0,7},{9,8},{10,9},{11,1... | collective-permute-start | bytes 30728 | tf_op jit(solution)/shard_map/ppermute | solution.py:47
  138.4 6.4 %collective-permute-start.2 = (f32[10,2,1,128]{3,2,1,0:T(1,128)S(1)}, f32[10,2,1,128]{3,2,1,0:T(1,128)S(1)}, u32[]{:S(2)}, u32[]{:S(2)}) collective-permute-start(f32[10,2,1,128]{3,2,1,0:T(1,128)S(1)} %get-tuple-element.707), channel_id=1, source_target_pairs={{0,1},{1,2},{2,3},{3,4},{4,5},{5,6},{6,7},{7,0},{8,9},{9,10},{10,1... | collective-permute-start | bytes 30728 | tf_op jit(solution)/shard_map/ppermute | solution.py:44
  184.8 3.5 %collective-permute-start.4 = (f32[10,1,8,128]{3,2,1,0:T(8,128)S(1)}, f32[10,1,8,128]{3,2,1,0:T(8,128)S(1)}, u32[]{:S(2)}, u32[]{:S(2)}) collective-permute-start(f32[10,1,8,128]{3,2,1,0:T(8,128)S(1)} %get-tuple-element.703), channel_id=1, source_target_pairs={{0,8},{8,16},{16,24},{24,0},{1,9},{9,17},{17,25},{25,1},{2,10},{10... | collective-permute-start | bytes 122888 | tf_op jit(solution)/shard_map/ppermute | solution.py:44
  184.8 3.5 %collective-permute-start.5 = (f32[10,1,8,128]{3,2,1,0:T(8,128)S(1)}, f32[10,1,8,128]{3,2,1,0:T(8,128)S(1)}, u32[]{:S(2)}, u32[]{:S(2)}) collective-permute-start(f32[10,1,8,128]{3,2,1,0:T(8,128)S(1)} %get-tuple-element.702), channel_id=1, source_target_pairs={{8,0},{16,8},{24,16},{0,24},{9,1},{17,9},{25,17},{1,25},{10,2},{18... | collective-permute-start | bytes 122888 | tf_op jit(solution)/shard_map/ppermute | solution.py:47
  188.4 6.4 %collective-permute-start.6 = (f32[10,2,1,128]{3,2,1,0:T(1,128)S(1)}, f32[10,2,1,128]{3,2,1,0:T(1,128)S(1)}, u32[]{:S(2)}, u32[]{:S(2)}) collective-permute-start(f32[10,2,1,128]{3,2,1,0:T(1,128)S(1)} %get-tuple-element.701), channel_id=1, source_target_pairs={{0,1},{1,2},{2,3},{3,4},{4,5},{5,6},{6,7},{7,0},{8,9},{9,10},{10,1... | collective-permute-start | bytes 30728 | tf_op jit(solution)/shard_map/ppermute | solution.py:44
  189.5 6.1 %collective-permute-start.7 = (f32[10,2,1,128]{3,2,1,0:T(1,128)S(1)}, f32[10,2,1,128]{3,2,1,0:T(1,128)S(1)}, u32[]{:S(2)}, u32[]{:S(2)}) collective-permute-start(f32[10,2,1,128]{3,2,1,0:T(1,128)S(1)} %get-tuple-element.700), channel_id=1, source_target_pairs={{1,0},{2,1},{3,2},{4,3},{5,4},{6,5},{7,6},{0,7},{9,8},{10,9},{11,1... | collective-permute-start | bytes 30728 | tf_op jit(solution)/shard_map/ppermute | solution.py:47
  196.7 0.7 copy-start.6
where the time goes:
time: 198 us; the launch traced here: 197 us
  blocking collectives  157 us (79%)
  starting transfers between devices  10.5 us (5%)
  waiting for transfers between devices  8.68 us (4%)
  matrix products  7.56 us (4%)
  other arithmetic  5.99 us (3%)
  local copies, waits for them, and re-layouts  5.31 us (3%)
    psum x2, blocking collectives, per_device(): velocity = lax.psum(partial_velocity, 'trans')  66 us
    all_gather x1, blocking collectives, per_device(): lax.all_gather(target, 'trans', axis=1, tiled=True)  26.2 us
    all_gather x1, blocking collectives, per_device(): lax.all_gather(fractions, 'trans', axis=1, tiled=True)  26.1 us
    all_gather x1, blocking collectives, per_device(): lax.all_gather(support, 'trans', axis=0, tiled=True)  22.3 us
    all_gather x1, blocking collectives, per_device(): lax.all_gather(area, 'trans', axis=0, tiled=True)  16.4 us
    ppermute x4, starting transfers between devices, extended(): lax.ppermute(lax.slice_in_dim(block, 0, width, axis=dim), axis, backward)  8.28 us
    ppermute x4, waiting for transfers between devices, extended(): lax.ppermute(lax.slice_in_dim(block, block.shape[dim] - width, None, axis...  6.68 us
    dot_general x8, matrix products, interpolate(): jnp.einsum('mp,cpd->cmd', pair_weight, velocity_field, precision=lax.Prec...  4.27 us
  transfers between devices with their start and end apart: 8, of which 7 were waited for; matrix products, arithmetic and copies ran while one was open for 1% of the time, Pallas kernels for 0%

commit v1 on v0

v1 whole, which is shorter than its diff:
```python
import math

import jax
import jax.numpy as jnp
from jax import lax
from jax.experimental import pallas as pl
from jax.experimental.pallas import tpu as pltpu
from jax.sharding import PartitionSpec as P

STEPS = 2
HALO = 4

velocity_table = (
    (0, 0, 0),
    (1, 0, 0),
    (-1, 0, 0),
    (0, 1, 0),
    (0, -1, 0),
    (0, 0, 1),
    (0, 0, -1),
    (1, 1, 0),
    (-1, -1, 0),
    (1, -1, 0),
    (-1, 1, 0),
    (1, 0, 1),
    (-1, 0, -1),
    (1, 0, -1),
    (-1, 0, 1),
    (0, 1, 1),
    (0, -1, -1),
    (0, 1, -1),
    (0, -1, 1),
)
weight_table = (1.0 / 3.0,) + (1.0 / 18.0,) * 6 + (1.0 / 36.0,) * 12
relax_base = 0.8
smagorinsky = 0.17
forward_x = tuple(i for i in range(19) if velocity_table[i][0] == 1)
backward_x = tuple(i for i in range(19) if velocity_table[i][0] == -1)
pairs = tuple((i, i + 1) for i in range(1, 19, 2))


def signed_sum(factors, values):
    running = None
    for factor, value in zip(factors, values):
        if factor != 0:
            if running is None:
                running = value if factor > 0 else -value
            else:
                running = running + value if factor > 0 else running - value
    return running


def tree_sum(values):
    values = list(values)
    while len(values) > 1:
        values = [
            values[k] + values[k + 1] if k + 1 < len(values) else values[k]
            for k in range(0, len(values), 2)
        ]
    return values[0]


def moments(f):
    plus = {i: f[i] + f[j] for i, j in pairs}
    minus = {i: f[i] - f[j] for i, j in pairs}
    density = tree_sum([f[0]] + [plus[i] for i, _ in pairs])
    momenta = []
    for d in range(3):
        momenta.append(
            signed_sum(
                [velocity_table[i][d] for i, _ in pairs], [minus[i] for i, _ in pairs]
            )
        )
    second = {}
    for a, b in ((0, 0), (1, 1), (2, 2), (0, 1), (0, 2), (1, 2)):
        second[(a, b)] = signed_sum(
            [velocity_table[i][a] * velocity_table[i][b] for i, _ in pairs],
            [plus[i] for i, _ in pairs],
        )
    return density, momenta, second


def collide(f, density, momenta, second, force, solid):
    inverse = 1.0 / density
    u = [(momenta[d] + 0.5 * force[d]) * inverse for d in range(3)]
    square = u[0] * u[0] + u[1] * u[1] + u[2] * u[2]
    along = u[0] * force[0] + u[1] * force[1] + u[2] * force[2]
    magnitude = None
    third = density * (1.0 / 3.0)
    for a, b in ((0, 0), (1, 1), (2, 2), (0, 1), (0, 2), (1, 2)):
        part = second[(a, b)] - density * (u[a] * u[b])
        if a == b:
            part = part - third
            term = part * part
        else:
            term = 2.0 * part * part
        magnitude = term if magnitude is None else magnitude + term
    magnitude = jnp.sqrt(magnitude)
    tau = 0.5 * (
        relax_base
        + jnp.sqrt(
            relax_base * relax_base
            + (18.0 * math.sqrt(2.0) * smagorinsky * smagorinsky) * magnitude * inverse
        )
    )
    omega = 1.0 / tau
    keep = 1.0 - omega
    share = 1.0 - 0.5 * omega
    scaled = omega * density
    q = [scaled * u[d] + share * force[d] for d in range(3)]
    base = scaled * (1.0 - 1.5 * square) - 3.0 * share * along
    out = [None] * 19
    out[0] = jnp.where(solid, f[0], keep * f[0] + weight_table[0] * base)
    for i, j in pairs:
        c = velocity_table[i]
        p = signed_sum(c, u)
        cq = signed_sum(c, q)
        w = weight_table[i]
        even = w * (base + 9.0 * p * (cq - 0.5 * scaled * p))
        odd = (3.0 * w) * cq
        out[i] = jnp.where(solid, f[j], keep * f[i] + (even + odd))
        out[j] = jnp.where(solid, f[i], keep * f[j] + (even - odd))
    return out


def split_pieces(value):
    high = value.astype(jnp.bfloat16)
    low = (value - high.astype(jnp.float32)).astype(jnp.bfloat16)
    return high, low


def marker_pass(velocity, marker_ref, row_start, row_count, total_rows, depth_count):
    planes, rows, depth = velocity[0].shape
    cells = planes * rows
    blocks = marker_ref.shape[0]
    width = marker_ref.shape[2]
    stacked = jnp.concatenate([v.reshape(cells, depth) for v in velocity], axis=0)
    shifted = pltpu.roll(stacked, depth - 1, 1)
    high, low = split_pieces(stacked)
    high_next, low_next = split_pieces(shifted)
    left = jnp.concatenate(
        [
            jnp.concatenate([high, low], axis=1),
            jnp.concatenate([high_next, low_next], axis=1),
        ],
        axis=0,
    )
    group = 2 if blocks % 2 == 0 else 1
    lanes = group * width
    row_iota = lax.broadcasted_iota(jnp.int32, (rows, lanes), 0)
    relative = jnp.where(row_iota < rows - HALO, row_iota, row_iota - rows)
    row_id = relative + row_start
    row_id = jnp.where(row_id < 0, row_id + total_rows, row_id)
    row_id = jnp.where(row_id >= total_rows, row_id - total_rows, row_id)
    depth_iota = lax.broadcasted_iota(jnp.int32, (depth, lanes), 0)
    total = None
    owned = []
    for start in range(0, blocks, group):
        parts = [marker_ref[start + k] for k in range(group)]
        data = parts[0] if group == 1 else jnp.concatenate(parts, axis=1)
        cell = data[0:1].astype(jnp.int32)
        column = cell // depth_count
        place = cell - column * depth_count
        fx, fy, fz = data[1:2], data[2:3], data[3:4]
        area = data[7:8]
        selector = jnp.where(depth_iota == place, 1.0, 0.0).astype(jnp.bfloat16)
        both = jnp.concatenate([selector, selector], axis=0)
        gathered = lax.dot_general(
            left, both, (((1,), (0,)), ((), ())), preferred_element_type=jnp.float32
        )
        row_weight = jnp.where(row_id == column, 1.0 - fy, 0.0) + jnp.where(
            row_id == column + 1, fy, 0.0
        )
        pair_weight = jnp.concatenate([row_weight * (1.0 - fx), row_weight * fx], axis=0)
        near = pair_weight * (1.0 - fz)
        far = pair_weight * fz
        offset = column - row_start
        own = jnp.logical_and(offset >= 0, offset < row_count)
        force = []
        for c in range(3):
            terms = near * gathered[c * cells : (c + 1) * cells] + far * gathered[
                (3 + c) * cells : (4 + c) * cells
            ]
            value = jnp.sum(terms, axis=0, keepdims=True)
            force.append(area * (data[4 + c : 5 + c] - value))
        owned.append([jnp.where(own, value, 0.0) for value in force])
        spread = jnp.concatenate(
            [near * value for value in force] + [far * value for value in force], axis=0
        )
        spread_high, spread_low = split_pieces(spread)
        added = lax.dot_general(
            jnp.concatenate([spread_high, spread_low], axis=0),
            selector,
            (((1,), (1,)), ((), ())),
            preferred_element_type=jnp.float32,
        )
        total = added if total is None else total + added
    near_part = total[0 : 3 * cells] + total[6 * cells : 9 * cells]
    far_part = total[3 * cells : 6 * cells] + total[9 * cells : 12 * cells]
    grid = near_part + pltpu.roll(far_part, 1, 1)
    forcing = [
        grid[c * cells : (c + 1) * cells].reshape(planes, rows, depth) for c in range(3)
    ]
    return forcing, owned, group, width


def moved(value, member):
    _, step_y, step_z = velocity_table[member]
    if step_y:
        value = pltpu.roll(value, step_y % value.shape[1], 1)
    if step_z:
        value = pltpu.roll(value, step_z % value.shape[2], 2)
    return value


def first_kernel(own_ref, after_ref, before_ref, solid_ref, marker_ref, start_ref,
                 next_ref, up_ref, down_ref, solid_out_ref, window,
                 *, total_rows, depth_count):
    row_count = own_ref.shape[2]
    window[0:19, :, 0:row_count, :] = own_ref[...]
    window[19, :, 0:row_count, :] = solid_ref[...].astype(jnp.float32)
    window[:, :, row_count : row_count + HALO, :] = after_ref[...]
    window[:, :, row_count + HALO :, :] = before_ref[...]
    f = [window[i] for i in range(19)]
    solid_values = window[19]
    solid_out_ref[...] = solid_values
    density, momenta, second = moments(f)
    inverse = 1.0 / density
    velocity = [m * inverse for m in momenta]
    row_start = start_ref[0]
    forcing, _, _, _ = marker_pass(
        velocity, marker_ref, row_start, row_count, total_rows, depth_count
    )
    out = collide(f, density, momenta, second, forcing, solid_values == 1.0)
    for i in range(19):
        value = moved(out[i], i)
        step_x = velocity_table[i][0]
        if step_x == 0:
            next_ref[i] = value
        elif step_x == 1:
            next_ref[i, 1] = value[0]
            up_ref[forward_x.index(i)] = value[1]
        else:
            next_ref[i, 0] = value[1]
            down_ref[backward_x.index(i)] = value[0]


def last_kernel(next_ref, low_ref, high_ref, solid_ref, marker_ref, start_ref,
                out_ref, up_ref, down_ref, force_ref,
                *, row_count, total_rows, depth_count):
    f = []
    for i in range(19):
        step_x = velocity_table[i][0]
        if step_x == 0:
            f.append(next_ref[i])
        elif step_x == 1:
            f.append(jnp.stack([low_ref[forward_x.index(i)], next_ref[i, 1]]))
        else:
            f.append(jnp.stack([next_ref[i, 0], high_ref[backward_x.index(i)]]))
    density, momenta, second = moments(f)
    inverse = 1.0 / density
    velocity = [m * inverse for m in momenta]
    row_start = start_ref[0]
    forcing, owned, group, width = marker_pass(
        velocity, marker_ref, row_start, row_count, total_rows, depth_count
    )
    for position, values in enumerate(owned):
        for k in range(group):
            for c in range(3):
                force_ref[position * group + k, c : c + 1, :] = values[c][
                    :, k * width : (k + 1) * width
                ]
    out = collide(f, density, momenta, second, forcing, solid_ref[...] == 1.0)
    for i in range(19):
        value = moved(out[i], i)[:, 0:row_count]
        step_x = velocity_table[i][0]
        if step_x == 0:
            out_ref[i] = value
        elif step_x == 1:
            out_ref[i, 1] = value[0]
            up_ref[forward_x.index(i)] = value[1]
        else:
            out_ref[i, 0] = value[1]
            down_ref[backward_x.index(i)] = value[0]


def ring(count, step):
    return [(i, (i + step) % count) for i in range(count)]


def exchanged(low_bound, high_bound, axis):
    count = lax.axis_size(axis)
    from_low = lax.ppermute(high_bound, axis, ring(count, 1))
    from_high = lax.ppermute(low_bound, axis, ring(count, -1))
    return from_low, from_high


def per_device(populations, solid, support, fractions, target, area):
    plane_count, row_count, depth_count = populations.shape[1:]
    own_markers = support.shape[0]
    groups = lax.axis_size("trans")
    total_rows = row_count * groups
    rows = row_count + 2 * HALO
    row_start = (lax.axis_index("trans") * row_count).astype(jnp.int32).reshape(1)

    packed = jnp.concatenate(
        [support.astype(jnp.float32)[None], fractions, target, area[None]], axis=0
    )
    rim = jnp.concatenate([populations, solid.astype(jnp.float32)[None]], axis=0)
    before, after = exchanged(
        rim[:, :, :HALO], rim[:, :, row_count - HALO :], "trans"
    )
    copies = jnp.broadcast_to(packed[None], (groups,) + packed.shape)
    markers = lax.all_to_all(copies, "trans", 0, 0, tiled=False)

    vmem = pl.BlockSpec(memory_space=pltpu.VMEM)
    smem = pl.BlockSpec(memory_space=pltpu.SMEM)
    f32 = jnp.float32
    side = len(forward_x)

    def first(*refs):
        first_kernel(*refs, total_rows=total_rows, depth_count=depth_count)

    following, up, down, solid_window = pl.pallas_call(
        first,
        out_shape=(
            jax.ShapeDtypeStruct((19, plane_count, rows, depth_count), f32),
            jax.ShapeDtypeStruct((side, rows, depth_count), f32),
            jax.ShapeDtypeStruct((side, rows, depth_count), f32),
            jax.ShapeDtypeStruct((plane_count, rows, depth_count), f32),
        ),
        in_specs=[vmem, vmem, vmem, vmem, vmem, smem],
        out_specs=(vmem, vmem, vmem, vmem),
        scratch_shapes=[pltpu.VMEM((20, plane_count, rows, depth_count), f32)],
        name="first_step",
    )(populations, after, before, solid, markers, row_start)
    from_low, from_high = exchanged(down, up, "stream")

    def last(*refs):
        last_kernel(*refs, row_count=row_count, total_rows=total_rows, depth_count=depth_count)

    outgoing, up, down, force = pl.pallas_call(
        last,
        out_shape=(
            jax.ShapeDtypeStruct((19, plane_count, row_count, depth_count), f32),
            jax.ShapeDtypeStruct((side, row_count, depth_count), f32),
            jax.ShapeDtypeStruct((side, row_count, depth_count), f32),
            jax.ShapeDtypeStruct((groups, 3, own_markers), f32),
        ),
        in_specs=[vmem, vmem, vmem, vmem, vmem, smem],
        out_specs=(vmem, vmem, vmem, vmem),
        name="last_step",
    )(following, from_low, from_high, solid_window, markers, row_start)
    from_low, from_high = exchanged(down, up, "stream")
    own_force = jnp.sum(lax.all_to_all(force, "trans", 0, 0, tiled=False), axis=0)
    planes = []
    for i in range(19):
        step_x = velocity_table[i][0]
        if step_x == 0:
            planes.append(outgoing[i])
        elif step_x == 1:
            planes.append(jnp.stack([from_low[forward_x.index(i)], outgoing[i, 1]]))
        else:
            planes.append(jnp.stack([outgoing[i, 0], from_high[backward_x.index(i)]]))
    return (jnp.stack(planes), own_force)


def solution(mesh):
    placed = (
        P(None, "stream", "trans", None),
        P("stream", "trans", None),
        P(("stream", "trans")),
        P(None, ("stream", "trans")),
        P(None, ("stream", "trans")),
        P(("stream", "trans")),
    )
    return jax.shard_map(
        per_device,
        mesh=mesh,
        in_specs=placed,
        out_specs=(P(None, "stream", "trans", None), P(None, ("stream", "trans"))),
        check_vma=False,
    )
```

time: 198 us -> 45 us (0.23)
  blocking collectives: 157 us -> 0 us
  matrix products: 7.56 us -> 0 us
  starting transfers between devices: 10.5 us -> 16.5 us
  Pallas kernels: 0 us -> 5.8 us
  waiting for transfers between devices: 8.68 us -> 13.3 us
  other arithmetic: 5.99 us -> 2.36 us
    all_gather x4 -> x0, blocking collectives: 91 us -> none  [the longest x1 26.2 us: per_device(): lax.all_gather(target, 'trans', axis=1, tiled=True)]
    psum x2 -> x0, blocking collectives: 66 us -> none  [per_device(): velocity = lax.psum(partial_velocity, 'trans')]
    all_to_all x0 -> x2, waiting for transfers between devices: none -> 9.88 us  [the longest x1 6.62 us: per_device(): markers = lax.all_to_all(copies, 'trans', 0, 0, tiled=False)]
    dot_general x16 -> x0, matrix products: 7.56 us -> none  [the longest x8 4.27 us: interpolate(): jnp.einsum('mp,cpd->cmd', pair_weight, velocity_field, precision=lax.Prec...]
    all_to_all x0 -> x2, starting transfers between devices: none -> 6.81 us  [the longest x1 3.47 us: per_device(): lax.all_to_all(force, 'trans', 0, 0, tiled=False)]
    pallas_call x0 -> x2, Pallas kernels: none -> 5.8 us  [the longest x1 2.97 us: per_device(): pl.pallas_call(first, out_shape=(jax.ShapeDtypeStruct((19, plane_count, r...]
    ppermute x8 -> x6, waiting for transfers between devices: 8.68 us -> 3.47 us  [the longest x3 1.9 us: exchanged(): from_low = lax.ppermute(high_bound, axis, ring(count, 1))]
    add x32 -> x0, other arithmetic: 2.04 us -> none  [the longest x16 1.84 us: weight_tables(): jnp.where(depth_iota[None, :] == depth_index[:, None], (1.0 - block_fract...]
  transfers between devices with their start and end apart: 8 -> 8, of which waited for: 7 -> 5; matrix products, arithmetic and copies ran while one was open for 1% -> 8% of each run, Pallas kernels for 0% -> 0%
where the time goes in v1:
time: 45 us; the launch traced here: 44.4 us
  starting transfers between devices  16.5 us (37%)
  waiting for transfers between devices  13.3 us (30%)
  Pallas kernels  5.8 us (13%)
  local copies, waits for them, and re-layouts  5.6 us (12%)
  other arithmetic  2.36 us (5%)
  between operations  0.76 us (2%)
    all_to_all x1, waiting for transfers between devices, per_device(): markers = lax.all_to_all(copies, 'trans', 0, 0, tiled=False)  6.62 us
    ppermute x3, starting transfers between devices, exchanged(): from_high = lax.ppermute(low_bound, axis, ring(count, -1))  5.02 us
    ppermute x3, starting transfers between devices, exchanged(): from_low = lax.ppermute(high_bound, axis, ring(count, 1))  4.67 us
    all_to_all x1, starting transfers between devices, per_device(): lax.all_to_all(force, 'trans', 0, 0, tiled=False)  3.47 us
    unnamed x24, local copies, waits for them, and re-layouts  3.38 us
    all_to_all x1, starting transfers between devices, per_device(): markers = lax.all_to_all(copies, 'trans', 0, 0, tiled=False)  3.34 us
    all_to_all x1, waiting for transfers between devices, per_device(): lax.all_to_all(force, 'trans', 0, 0, tiled=False)  3.26 us
    pallas_call x1, Pallas kernels, per_device(): pl.pallas_call(first, out_shape=(jax.ShapeDtypeStruct((19, plane_count, r...  2.97 us
  transfers between devices with their start and end apart: 8, of which 5 were waited for; matrix products, arithmetic and copies ran while one was open for 8% of the time, Pallas kernels for 0%

profile of v1, /device:TPU:0, one launch (start us, length us, event | category | flops | bytes accessed | tf_op | source)
XLA Modules:
  0.0 44.4 jit_solution(7322355758575148830)
XLA Ops:
  0.6 0.7 %convert_bitcast_fusion = f32[1,2,8,128]{3,2,1,0:T(8,128)S(1)} fusion(s32[2,8,128]{2,1,0:T(8,128)} %refs_3_.1), kind=kLoop, calls=%fused_computation.27 | loop fusion | flops 2048 | bytes 16384 | tf_op jit(solution)/shard_map/broadcast_in_dim | solution.py:309
  1.3 1.0 %pad_maximum_fusion = (f32[20,2,4,128]{3,2,1,0:T(4,128)S(1)}, f32[20,2,4,128]{3,2,1,0:T(4,128)S(1)}) fusion(f32[1,2,8,128]{3,2,1,0:T(8,128)S(1)} %convert_bitcast_fusion, f32[19,2,8,128]{3,2,1,0:T(8,128)} %refs_0_.1), kind=kLoop, calls=%fused_computation.3 | loop fusion | flops 40960 | bytes 327680 | tf_op jit(solution)/shard_map/concatenate | solution.py:309
  2.4 0.0 copy-start.10
  2.4 3.0 %collective-permute-start.1 = (f32[20,2,4,128]{3,2,1,0:T(4,128)S(1)}, f32[20,2,4,128]{3,2,1,0:T(4,128)S(1)}, u32[]{:S(2)}, u32[]{:S(2)}) collective-permute-start(f32[20,2,4,128]{3,2,1,0:T(4,128)S(1)} %get-tuple-element.18), channel_id=1, source_target_pairs={{0,1},{1,2},{2,3},{3,4},{4,5},{5,6},{6,7},{7,0},{8,9},{9,10},{10,1... | collective-permute-start | bytes 245768 | tf_op jit(solution)/shard_map/ppermute | solution.py:293
  5.4 3.1 %collective-permute-start = (f32[20,2,4,128]{3,2,1,0:T(4,128)S(1)}, f32[20,2,4,128]{3,2,1,0:T(4,128)S(1)}, u32[]{:S(2)}, u32[]{:S(2)}) collective-permute-start(f32[20,2,4,128]{3,2,1,0:T(4,128)S(1)} %get-tuple-element.19), channel_id=1, source_target_pairs={{0,7},{1,0},{2,1},{3,2},{4,3},{5,4},{6,5},{7,6},{8,15},{9,8},{10,9... | collective-permute-start | bytes 245768 | tf_op jit(solution)/shard_map/ppermute | solution.py:294
  8.5 0.6 %copy-done.7 = f32[128]{0:T(128)S(1)} copy-done((f32[128]{0:T(128)S(1)}, f32[128]{0:T(128)}, u32[]{:S(2)}) %copy-start.7) | copy-done | bytes 536
  9.2 0.6 %broadcast_in_dim.18 = f32[8,8,128]{2,1,0:T(8,128)} broadcast(f32[8,128]{1,0:T(8,128)S(1)} %pad_maximum_fusion.1), dimensions={1,2} | broadcast | bytes 36864 | tf_op jit(solution)/shard_map/broadcast_in_dim | solution.py:313
  9.8 3.3 %all-to-all-start = ((f32[8,8,128]{2,1,0:T(8,128)}), f32[8,8,128]{2,1,0:T(8,128)S(1)}, u32[]{:S(2)}, u32[]{:S(2)}) async-start(f32[8,8,128]{2,1,0:T(8,128)} %broadcast_in_dim.18), calls=%async_computation | async-start | bytes 65536 | tf_op jit(solution)/shard_map/all_to_all | solution.py:314
  13.2 6.6 %all-to-all-done.refs_4_ = f32[8,8,128]{2,1,0:T(8,128)S(1)} async-done(((f32[8,8,128]{2,1,0:T(8,128)}), f32[8,8,128]{2,1,0:T(8,128)S(1)}, u32[]{:S(2)}, u32[]{:S(2)}) %all-to-all-start) | async-done | bytes 32800 | tf_op jit(solution)/shard_map/all_to_all | solution.py:314
  19.8 0.0 collective-permute-done.1.refs_2_
  19.8 0.0 copy-start.2
  19.8 0.6 %copy-done = f32[8,8,128]{2,1,0:T(8,128)} copy-done((f32[8,8,128]{2,1,0:T(8,128)}, f32[8,8,128]{2,1,0:T(8,128)S(1)}, u32[]{:S(2)}) %copy-start) | copy-done | bytes 32792
  20.4 0.0 copy-done.1
  20.4 0.0 copy-done.2
  20.4 3.0 %first_step.1 = (f32[19,2,16,128]{3,2,1,0:T(8,128)}, f32[5,16,128]{2,1,0:T(8,128)}, f32[5,16,128]{2,1,0:T(8,128)}, f32[2,16,128]{2,1,0:T(8,128)}) custom-call(f32[19,2,8,128]{3,2,1,0:T(8,128)} %refs_0_.1, f32[20,2,4,128]{3,2,1,0:T(4,128)} %copy-done.2, f32[20,2,4,128]{3,2,1,0:T(4,128)} %copy-done.1, s32[2,8,128]{2,1,0:T(8,128)} %refs_3_.1, ...), custom_call_target="tpu_custom_call" | custom-call | tf_op jit(solution)/shard_map/first_step/pallas_call | solution.py:324
  23.4 0.0 collective-permute-start.2
  23.4 1.7 %collective-permute-start.3 = (f32[5,16,128]{2,1,0:T(8,128)}, f32[5,16,128]{2,1,0:T(8,128)S(1)}, u32[]{:S(2)}, u32[]{:S(2)}) collective-permute-start(f32[5,16,128]{2,1,0:T(8,128)} %get-tuple-element.12), channel_id=1, source_target_pairs={{0,24},{8,0},{16,8},{24,16},{1,25},{9,1},{17,9},{25,17},{2,26},{10... | collective-permute-start | bytes 122888 | tf_op jit(solution)/shard_map/ppermute | solution.py:294
  25.2 1.9 %collective-permute-done.2.refs_1_ = f32[5,16,128]{2,1,0:T(8,128)S(1)} collective-permute-done((f32[5,16,128]{2,1,0:T(8,128)}, f32[5,16,128]{2,1,0:T(8,128)S(1)}, u32[]{:S(2)}, u32[]{:S(2)}) %collective-permute-start.2) | collective-permute-done | bytes 40992 | tf_op jit(solution)/shard_map/ppermute | solution.py:293
  27.1 0.1 collective-permute-done.3.refs_2_
  27.2 0.5 %copy-done.3 = f32[5,16,128]{2,1,0:T(8,128)} copy-done((f32[5,16,128]{2,1,0:T(8,128)}, f32[5,16,128]{2,1,0:T(8,128)S(1)}, u32[]{:S(2)}) %copy-start.3) | copy-done | bytes 40984
  27.7 0.1 copy-done.4
  27.8 2.8 %last_step.1 = (f32[19,2,8,128]{3,2,1,0:T(8,128)}, f32[5,8,128]{2,1,0:T(8,128)}, f32[5,8,128]{2,1,0:T(8,128)}, f32[8,3,128]{2,1,0:T(4,128)}) custom-call(f32[19,2,16,128]{3,2,1,0:T(8,128)} %get-tuple-element.10.refs_0_, f32[5,16,128]{2,1,0:T(8,128)} %copy-done.3, f32[5,16,128]{2,1,0:T(8,128)} %copy-done.4, f32[2,16,128]{2,1,0:T(8,128)} %get-tuple-element.13.refs_3_, ...), custom_call_target="tpu_custom_call" | custom-call | tf_op jit(solution)/shard_map/last_step/pallas_call | solution.py:342
  30.6 1.6 %collective-permute-start.4 = (f32[5,8,128]{2,1,0:T(8,128)}, f32[5,8,128]{2,1,0:T(8,128)S(1)}, u32[]{:S(2)}, u32[]{:S(2)}) collective-permute-start(f32[5,8,128]{2,1,0:T(8,128)} %get-tuple-element.15), channel_id=1, source_target_pairs={{0,8},{8,16},{16,24},{24,0},{1,9},{9,17},{17,25},{25,1},{2,10},{10... | collective-permute-start | bytes 61448 | tf_op jit(solution)/shard_map/ppermute | solution.py:293
  32.2 0.8 %slice_bitcast_fusion = (f32[1,8,128]{2,1,0:T(8,128)S(1)}, f32[1,8,128]{2,1,0:T(8,128)S(1)}, f32[1,8,128]{2,1,0:T(8,128)S(1)}, f32[1,8,128]{2,1,0:T(8,128)S(1)},...) fusion(f32[19,2,8,128]{3,2,1,0:T(8,128)} %get-tuple-element.14), kind=kLoop, calls=%fused_computation.29 | loop fusion | bytes 81920 | tf_op jit(solution)/shard_map/stack;squeeze | solution.py:364
  33.1 0.7 %constant_dynamic-update-slice_fusion.10 = f32[19,2,8,128]{3,2,1,0:T(8,128)S(1)} fusion(f32[19,2,8,128]{3,2,1,0:T(8,128)} %get-tuple-element.14), kind=kLoop, calls=%fused_computation.16 | loop fusion | bytes 16384
  33.8 3.5 %all-to-all-start.1 = ((f32[8,3,128]{2,1,0:T(4,128)}), f32[8,3,128]{2,1,0:T(4,128)S(1)}, u32[]{:S(2)}, u32[]{:S(2)}) async-start(f32[8,3,128]{2,1,0:T(4,128)} %get-tuple-element.17), calls=%async_computation.1 | async-start | bytes 32768 | tf_op jit(solution)/shard_map/all_to_all | solution.py:355
  37.3 0.2 collective-permute-start.5
  37.4 1.5 %collective-permute-done.5 = f32[5,8,128]{2,1,0:T(8,128)S(1)} collective-permute-done((f32[5,8,128]{2,1,0:T(8,128)S(1)}, f32[5,8,128]{2,1,0:T(8,128)S(1)}, u32[]{:S(2)}, u32[]{:S(2)}) %collective-permute-start.5) | collective-permute-done | bytes 20512 | tf_op jit(solution)/shard_map/ppermute | solution.py:294
  38.9 0.8 %slice_dynamic-update-slice_fusion.1 = f32[19,2,8,128]{3,2,1,0:T(8,128)S(1)} fusion(f32[19,2,8,128]{3,2,1,0:T(8,128)S(1)} %constant_dynamic-update-slice_fusion.8, f32[19,2,8,128]{3,2,1,0:T(8,128)} %get-tuple-element.14), kind=kLoop, calls=%fused_computation.5 | loop fusion | bytes 65536
  39.7 0.8 %slice_dynamic-update-slice_fusion = f32[19,2,8,128]{3,2,1,0:T(8,128)S(1)} fusion(f32[19,2,8,128]{3,2,1,0:T(8,128)S(1)} %constant_dynamic-update-slice_fusion, f32[19,2,8,128]{3,2,1,0:T(8,128)} %get-tuple-element.14), kind=kLoop, calls=%fused_computation.4 | loop fusion | bytes 65536 | tf_op jit(solution)/shard_map/stack | solution.py:365
  40.5 3.3 %all-to-all-done.1 = f32[8,3,128]{2,1,0:T(4,128)S(1)} async-done(((f32[8,3,128]{2,1,0:T(4,128)}), f32[8,3,128]{2,1,0:T(4,128)S(1)}, u32[]{:S(2)}, u32[]{:S(2)}) %all-to-all-start.1) | async-done | bytes 12320 | tf_op jit(solution)/shard_map/all_to_all | solution.py:355
  43.8 0.6 %reduce_sum.9 = f32[3,128]{1,0:T(4,128)} reduce(f32[8,3,128]{2,1,0:T(4,128)S(1)} %all-to-all-done.1, f32[]{:T(128)} %constant.2.clone.1), dimensions={0}, to_apply=%region_0.0 | reduce | flops 2688 | bytes 13828 | tf_op jit(solution)/shard_map/reduce_sum | solution.py:355
  (30 shorter events, 0.1 us)
Async XLA Ops:
  2.4 6.2 %copy-start.10 = (s32[128]{0:T(128)S(1)}, s32[128]{0:T(128)}, u32[]{:S(2)}) copy-start(s32[128]{0:T(128)} %param.8) | copy-start | bytes 1540
  2.4 17.4 %collective-permute-start.1 = (f32[20,2,4,128]{3,2,1,0:T(4,128)S(1)}, f32[20,2,4,128]{3,2,1,0:T(4,128)S(1)}, u32[]{:S(2)}, u32[]{:S(2)}) collective-permute-start(f32[20,2,4,128]{3,2,1,0:T(4,128)S(1)} %get-tuple-element.18), channel_id=1, source_target_pairs={{0,1},{1,2},{2,3},{3,4},{4,5},{5,6},{6,7},{7,0},{8,9},{9,10},{10,1... | collective-permute-start | bytes 245768 | tf_op jit(solution)/shard_map/ppermute | solution.py:293
  5.4 3.1 %copy-start.6 = (f32[3,128]{1,0:T(4,128)S(1)}, f32[3,128]{1,0:T(4,128)}, u32[]{:S(2)}) copy-start(f32[3,128]{1,0:T(4,128)} %param.9) | copy-start | bytes 4612
  5.4 3.1 %copy-start.5 = (f32[3,128]{1,0:T(4,128)S(1)}, f32[3,128]{1,0:T(4,128)}, u32[]{:S(2)}) copy-start(f32[3,128]{1,0:T(4,128)} %param.10) | copy-start | bytes 4612
  5.4 14.4 %collective-permute-start = (f32[20,2,4,128]{3,2,1,0:T(4,128)S(1)}, f32[20,2,4,128]{3,2,1,0:T(4,128)S(1)}, u32[]{:S(2)}, u32[]{:S(2)}) collective-permute-start(f32[20,2,4,128]{3,2,1,0:T(4,128)S(1)} %get-tuple-element.19), channel_id=1, source_target_pairs={{0,7},{1,0},{2,1},{3,2},{4,3},{5,4},{6,5},{7,6},{8,15},{9,8},{10,9... | collective-permute-start | bytes 245768 | tf_op jit(solution)/shard_map/ppermute | solution.py:294
  8.5 0.7 %copy-start.7 = (f32[128]{0:T(128)S(1)}, f32[128]{0:T(128)}, u32[]{:S(2)}) copy-start(f32[128]{0:T(128)} %param.11) | copy-start | bytes 1540
  9.8 10.0 %all-to-all-start = ((f32[8,8,128]{2,1,0:T(8,128)}), f32[8,8,128]{2,1,0:T(8,128)S(1)}, u32[]{:S(2)}, u32[]{:S(2)}) async-start(f32[8,8,128]{2,1,0:T(8,128)} %broadcast_in_dim.18), calls=%async_computation | async-start | bytes 65536 | tf_op jit(solution)/shard_map/all_to_all | solution.py:314
  19.8 0.6 %copy-start = (f32[8,8,128]{2,1,0:T(8,128)}, f32[8,8,128]{2,1,0:T(8,128)S(1)}, u32[]{:S(2)}) copy-start(f32[8,8,128]{2,1,0:T(8,128)S(1)} %all-to-all-done.refs_4_) | copy-start | bytes 98308
  19.8 0.6 %copy-start.1 = (f32[20,2,4,128]{3,2,1,0:T(4,128)}, f32[20,2,4,128]{3,2,1,0:T(4,128)S(1)}, u32[]{:S(2)}) copy-start(f32[20,2,4,128]{3,2,1,0:T(4,128)S(1)} %collective-permute-done.1.refs_2_) | copy-start | bytes 245764
  19.8 0.7 %copy-start.2 = (f32[20,2,4,128]{3,2,1,0:T(4,128)}, f32[20,2,4,128]{3,2,1,0:T(4,128)S(1)}, u32[]{:S(2)}) copy-start(f32[20,2,4,128]{3,2,1,0:T(4,128)S(1)} %collective-permute-done.refs_1_) | copy-start | bytes 245764
  23.4 3.6 %collective-permute-start.2 = (f32[5,16,128]{2,1,0:T(8,128)}, f32[5,16,128]{2,1,0:T(8,128)S(1)}, u32[]{:S(2)}, u32[]{:S(2)}) collective-permute-start(f32[5,16,128]{2,1,0:T(8,128)} %get-tuple-element.11), channel_id=1, source_target_pairs={{0,8},{8,16},{16,24},{24,0},{1,9},{9,17},{17,25},{25,1},{2,10},{10... | collective-permute-start | bytes 122888 | tf_op jit(solution)/shard_map/ppermute | solution.py:293
  23.4 3.7 %collective-permute-start.3 = (f32[5,16,128]{2,1,0:T(8,128)}, f32[5,16,128]{2,1,0:T(8,128)S(1)}, u32[]{:S(2)}, u32[]{:S(2)}) collective-permute-start(f32[5,16,128]{2,1,0:T(8,128)} %get-tuple-element.12), channel_id=1, source_target_pairs={{0,24},{8,0},{16,8},{24,16},{1,25},{9,1},{17,9},{25,17},{2,26},{10... | collective-permute-start | bytes 122888 | tf_op jit(solution)/shard_map/ppermute | solution.py:294
  27.1 0.6 %copy-start.3 = (f32[5,16,128]{2,1,0:T(8,128)}, f32[5,16,128]{2,1,0:T(8,128)S(1)}, u32[]{:S(2)}) copy-start(f32[5,16,128]{2,1,0:T(8,128)S(1)} %collective-permute-done.2.refs_1_) | copy-start | bytes 122884
  27.2 0.6 %copy-start.4 = (f32[5,16,128]{2,1,0:T(8,128)}, f32[5,16,128]{2,1,0:T(8,128)S(1)}, u32[]{:S(2)}) copy-start(f32[5,16,128]{2,1,0:T(8,128)S(1)} %collective-permute-done.3.refs_2_) | copy-start | bytes 122884
  30.6 6.8 %collective-permute-start.4 = (f32[5,8,128]{2,1,0:T(8,128)}, f32[5,8,128]{2,1,0:T(8,128)S(1)}, u32[]{:S(2)}, u32[]{:S(2)}) collective-permute-start(f32[5,8,128]{2,1,0:T(8,128)} %get-tuple-element.15), channel_id=1, source_target_pairs={{0,8},{8,16},{16,24},{24,0},{1,9},{9,17},{17,25},{25,1},{2,10},{10... | collective-permute-start | bytes 61448 | tf_op jit(solution)/shard_map/ppermute | solution.py:293
  33.8 3.5 %copy-start.9 = (f32[5,8,128]{2,1,0:T(8,128)S(1)}, f32[5,8,128]{2,1,0:T(8,128)}, u32[]{:S(2)}) copy-start(f32[5,8,128]{2,1,0:T(8,128)} %get-tuple-element.16) | copy-start | bytes 61444
  33.8 10.0 %all-to-all-start.1 = ((f32[8,3,128]{2,1,0:T(4,128)}), f32[8,3,128]{2,1,0:T(4,128)S(1)}, u32[]{:S(2)}, u32[]{:S(2)}) async-start(f32[8,3,128]{2,1,0:T(4,128)} %get-tuple-element.17), calls=%async_computation.1 | async-start | bytes 32768 | tf_op jit(solution)/shard_map/all_to_all | solution.py:355
  37.3 1.6 %collective-permute-start.5 = (f32[5,8,128]{2,1,0:T(8,128)S(1)}, f32[5,8,128]{2,1,0:T(8,128)S(1)}, u32[]{:S(2)}, u32[]{:S(2)}) collective-permute-start(f32[5,8,128]{2,1,0:T(8,128)S(1)} %copy-done.9), channel_id=1, source_target_pairs={{0,24},{8,0},{16,8},{24,16},{1,25},{9,1},{17,9},{25,17},{2,26},{10... | collective-permute-start | bytes 61448 | tf_op jit(solution)/shard_map/ppermute | solution.py:294
  40.5 3.9 %copy-start.8 = (f32[19,2,8,128]{3,2,1,0:T(8,128)}, f32[19,2,8,128]{3,2,1,0:T(8,128)S(1)}, u32[]{:S(2)}) copy-start(f32[19,2,8,128]{3,2,1,0:T(8,128)S(1)} %slice_dynamic-update-slice_fusion) | copy-start | bytes 466948

commit v2 on v1

v2 whole, which is shorter than its diff:
```python
import math

import jax
import jax.numpy as jnp
from jax import lax
from jax.experimental import pallas as pl
from jax.experimental.pallas import tpu as pltpu
from jax.sharding import PartitionSpec as P


HALO = 4

velocity_table = (
    (0, 0, 0),
    (1, 0, 0),
    (-1, 0, 0),
    (0, 1, 0),
    (0, -1, 0),
    (0, 0, 1),
    (0, 0, -1),
    (1, 1, 0),
    (-1, -1, 0),
    (1, -1, 0),
    (-1, 1, 0),
    (1, 0, 1),
    (-1, 0, -1),
    (1, 0, -1),
    (-1, 0, 1),
    (0, 1, 1),
    (0, -1, -1),
    (0, 1, -1),
    (0, -1, 1),
)
weight_table = (1.0 / 3.0,) + (1.0 / 18.0,) * 6 + (1.0 / 36.0,) * 12
relax_base = 0.8
smagorinsky = 0.17
forward_x = tuple(i for i in range(19) if velocity_table[i][0] == 1)
backward_x = tuple(i for i in range(19) if velocity_table[i][0] == -1)
pairs = tuple((i, i + 1) for i in range(1, 19, 2))


def signed_sum(factors, values):
    running = None
    for factor, value in zip(factors, values):
        if factor != 0:
            if running is None:
                running = value if factor > 0 else -value
            else:
                running = running + value if factor > 0 else running - value
    return running


def tree_sum(values):
    values = list(values)
    while len(values) > 1:
        values = [
            values[k] + values[k + 1] if k + 1 < len(values) else values[k]
            for k in range(0, len(values), 2)
        ]
    return values[0]


def moments(f):
    plus = {i: f[i] + f[j] for i, j in pairs}
    minus = {i: f[i] - f[j] for i, j in pairs}
    density = tree_sum([f[0]] + [plus[i] for i, _ in pairs])
    momenta = []
    for d in range(3):
        momenta.append(
            signed_sum(
                [velocity_table[i][d] for i, _ in pairs], [minus[i] for i, _ in pairs]
            )
        )
    second = {}
    for a, b in ((0, 0), (1, 1), (2, 2), (0, 1), (0, 2), (1, 2)):
        second[(a, b)] = signed_sum(
            [velocity_table[i][a] * velocity_table[i][b] for i, _ in pairs],
            [plus[i] for i, _ in pairs],
        )
    return density, momenta, second


def collide(f, density, momenta, second, force, solid):
    inverse = 1.0 / density
    u = [(momenta[d] + 0.5 * force[d]) * inverse for d in range(3)]
    square = u[0] * u[0] + u[1] * u[1] + u[2] * u[2]
    along = u[0] * force[0] + u[1] * force[1] + u[2] * force[2]
    magnitude = None
    third = density * (1.0 / 3.0)
    for a, b in ((0, 0), (1, 1), (2, 2), (0, 1), (0, 2), (1, 2)):
        part = second[(a, b)] - density * (u[a] * u[b])
        if a == b:
            part = part - third
            term = part * part
        else:
            term = 2.0 * part * part
        magnitude = term if magnitude is None else magnitude + term
    magnitude = jnp.sqrt(magnitude)
    tau = 0.5 * (
        relax_base
        + jnp.sqrt(
            relax_base * relax_base
            + (18.0 * math.sqrt(2.0) * smagorinsky * smagorinsky) * magnitude * inverse
        )
    )
    omega = 1.0 / tau
    keep = 1.0 - omega
    share = 1.0 - 0.5 * omega
    scaled = omega * density
    q = [scaled * u[d] + share * force[d] for d in range(3)]
    base = scaled * (1.0 - 1.5 * square) - 3.0 * share * along
    out = [None] * 19
    out[0] = jnp.where(solid, f[0], keep * f[0] + weight_table[0] * base)
    for i, j in pairs:
        c = velocity_table[i]
        p = signed_sum(c, u)
        cq = signed_sum(c, q)
        w = weight_table[i]
        even = w * (base + 9.0 * p * (cq - 0.5 * scaled * p))
        odd = (3.0 * w) * cq
        out[i] = jnp.where(solid, f[j], keep * f[i] + (even + odd))
        out[j] = jnp.where(solid, f[i], keep * f[j] + (even - odd))
    return out


def split_pieces(value):
    high = value.astype(jnp.bfloat16)
    low = (value - high.astype(jnp.float32)).astype(jnp.bfloat16)
    return high, low


class Markers:
    def __init__(self, marker_ref, row_start, rows, total_rows, depth):
        self.ref = marker_ref
        self.blocks = marker_ref.shape[0]
        self.width = marker_ref.shape[2]
        self.group = 2 if self.blocks % 2 == 0 else 1
        self.depth = depth
        lanes = self.group * self.width
        row_iota = lax.broadcasted_iota(jnp.int32, (rows, lanes), 0)
        relative = jnp.where(row_iota < rows - HALO, row_iota, row_iota - rows)
        row_id = relative + row_start
        row_id = jnp.where(row_id < 0, row_id + total_rows, row_id)
        self.row_id = jnp.where(row_id >= total_rows, row_id - total_rows, row_id)
        self.depth_iota = lax.broadcasted_iota(jnp.int32, (depth, lanes), 0)

    def starts(self):
        return range(0, self.blocks, self.group)

    def weights(self, start):
        parts = [self.ref[start + k] for k in range(self.group)]
        data = parts[0] if self.group == 1 else jnp.concatenate(parts, axis=1)
        cell = data[0:1].astype(jnp.int32)
        column = cell // self.depth
        place = cell - column * self.depth
        fx, fy, fz = data[1:2], data[2:3], data[3:4]
        selector = jnp.where(self.depth_iota == place, 1.0, 0.0).astype(jnp.bfloat16)
        row_weight = jnp.where(self.row_id == column, 1.0 - fy, 0.0) + jnp.where(
            self.row_id == column + 1, fy, 0.0
        )
        pair_weight = jnp.concatenate([row_weight * (1.0 - fx), row_weight * fx], axis=0)
        return data, column, selector, pair_weight * (1.0 - fz), pair_weight * fz


def velocity_operand(velocity):
    planes, rows, depth = velocity[0].shape
    stacked = jnp.concatenate([v.reshape(planes * rows, depth) for v in velocity], axis=0)
    shifted = pltpu.roll(stacked, depth - 1, 1)
    return jnp.concatenate(
        [
            jnp.concatenate(split_pieces(stacked), axis=1),
            jnp.concatenate(split_pieces(shifted), axis=1),
        ],
        axis=0,
    )


def marker_force(left, data, selector, near, far):
    cells = near.shape[0]
    gathered = lax.dot_general(
        left,
        jnp.concatenate([selector, selector], axis=0),
        (((1,), (0,)), ((), ())),
        preferred_element_type=jnp.float32,
    )
    force = []
    for c in range(3):
        terms = near * gathered[c * cells : (c + 1) * cells] + far * gathered[
            (3 + c) * cells : (4 + c) * cells
        ]
        value = jnp.sum(terms, axis=0, keepdims=True)
        force.append(data[7:8] * (data[4 + c : 5 + c] - value))
    return force


def spread_force(force, selector, near, far):
    spread = jnp.concatenate(
        [near * value for value in force] + [far * value for value in force], axis=0
    )
    return lax.dot_general(
        jnp.concatenate(split_pieces(spread), axis=0),
        selector,
        (((1,), (1,)), ((), ())),
        preferred_element_type=jnp.float32,
    )


def forcing_fields(total, planes, rows, depth):
    cells = planes * rows
    near = total[0 : 3 * cells] + total[6 * cells : 9 * cells]
    far = total[3 * cells : 6 * cells] + total[9 * cells : 12 * cells]
    grid = near + pltpu.roll(far, 1, 1)
    return [grid[c * cells : (c + 1) * cells].reshape(planes, rows, depth) for c in range(3)]


def moved(value, member):
    _, step_y, step_z = velocity_table[member]
    if step_y:
        value = pltpu.roll(value, step_y % value.shape[1], 1)
    if step_z:
        value = pltpu.roll(value, step_z % value.shape[2], 2)
    return value


def place_bits(place_ref):
    place = place_ref[0]
    return place >> 2, ((place >> 1) & 1) == 0, (place & 1) == 0


def pack_kernel(populations_hbm, solid_hbm, support_hbm, fractions_hbm, target_hbm, area_hbm,
                place_ref, packed_ref, own_ref, near_ref, far_ref,
                solid_buf, support_buf, fractions_buf, target_buf, area_buf, sems):
    small = [
        pltpu.make_async_copy(source, target, sems.at[k])
        for k, (source, target) in enumerate(
            (
                (support_hbm, support_buf),
                (fractions_hbm, fractions_buf),
                (target_hbm, target_buf),
                (area_hbm, area_buf),
            )
        )
    ]
    large = [
        pltpu.make_async_copy(solid_hbm, solid_buf, sems.at[4]),
        pltpu.make_async_copy(populations_hbm, own_ref.at[0:19], sems.at[5]),
    ]
    for copy in small + large:
        copy.start()
    for copy in small:
        copy.wait()
    packed_ref[0:1, :] = support_buf[...].astype(jnp.float32)
    packed_ref[1:4, :] = fractions_buf[...]
    packed_ref[4:7, :] = target_buf[...]
    packed_ref[7:8, :] = area_buf[...]
    for copy in large:
        copy.wait()
    own_ref[19] = solid_buf[...].astype(jnp.float32)
    _, even, _ = place_bits(place_ref)
    rows = own_ref.shape[2]
    for i in range(20):
        low = own_ref[i, :, 0:HALO, :]
        high = own_ref[i, :, rows - HALO :, :]
        near_ref[i] = jnp.where(even, high, low)
        far_ref[i] = jnp.where(even, low, high)


def store_moved(out, next_ref, near_ref, far_ref, even, rows):
    for k, (i, j) in enumerate(zip(forward_x, backward_x)):
        up = moved(out[i], i)[:, 0:rows]
        down = moved(out[j], j)[:, 0:rows]
        next_ref[i, 1] = up[0]
        next_ref[j, 0] = down[1]
        near_ref[k] = jnp.where(even, up[1], down[0])
        far_ref[k] = jnp.where(even, down[0], up[1])
    for i in range(19):
        if velocity_table[i][0] == 0:
            next_ref[i] = moved(out[i], i)[:, 0:rows]


def joined(next_ref, near_ref, far_ref, even):
    f = [None] * 19
    for k, (i, j) in enumerate(zip(forward_x, backward_x)):
        near, far = near_ref[k], far_ref[k]
        f[i] = jnp.stack([jnp.where(even, far, near), next_ref[i, 1]])
        f[j] = jnp.stack([next_ref[j, 0], jnp.where(even, near, far)])
    for i in range(19):
        if velocity_table[i][0] == 0:
            f[i] = next_ref[i]
    return f


def first_kernel(own_ref, rim_near_ref, rim_far_ref, marker_ref, place_ref,
                 next_ref, near_ref, far_ref, solid_out_ref, window, *, total_rows):
    row_count = own_ref.shape[2]
    _, planes, rows, depth = window.shape
    row_start, even, stream_even = place_bits(place_ref)
    window[:, :, 0:row_count, :] = own_ref[...]
    for i in range(20):
        near, far = rim_near_ref[i], rim_far_ref[i]
        window[i, :, row_count : row_count + HALO, :] = jnp.where(even, near, far)
        window[i, :, row_count + HALO :, :] = jnp.where(even, far, near)
    f = [window[i] for i in range(19)]
    solid_values = window[19]
    solid_out_ref[...] = solid_values
    density, momenta, second = moments(f)
    inverse = 1.0 / density
    left = velocity_operand([m * inverse for m in momenta])
    markers = Markers(marker_ref, row_start, rows, total_rows, depth)
    total = None
    for start in markers.starts():
        data, _, selector, near, far = markers.weights(start)
        force = marker_force(left, data, selector, near, far)
        added = spread_force(force, selector, near, far)
        total = added if total is None else total + added
    forcing = forcing_fields(total, planes, rows, depth)
    out = collide(f, density, momenta, second, forcing, solid_values == 1.0)
    store_moved(out, next_ref, near_ref, far_ref, stream_even, rows)


def force_kernel(next_ref, near_ref, far_ref, marker_ref, place_ref, force_ref, owned_ref,
                 *, row_count, total_rows):
    row_start, _, stream_even = place_bits(place_ref)
    f = joined(next_ref, near_ref, far_ref, stream_even)
    _, rows, depth = f[0].shape
    density, momenta, _ = moments(f)
    inverse = 1.0 / density
    left = velocity_operand([m * inverse for m in momenta])
    markers = Markers(marker_ref, row_start, rows, total_rows, depth)
    width = markers.width
    for start in markers.starts():
        data, column, selector, near, far = markers.weights(start)
        force = marker_force(left, data, selector, near, far)
        offset = column - row_start
        own = jnp.logical_and(offset >= 0, offset < row_count)
        for c in range(3):
            kept = jnp.where(own, force[c], 0.0)
            for k in range(markers.group):
                span = slice(k * width, (k + 1) * width)
                force_ref[start + k, c : c + 1, :] = force[c][:, span]
                owned_ref[start + k, c : c + 1, :] = kept[:, span]


def last_kernel(next_ref, near_in_ref, far_in_ref, solid_ref, marker_ref, force_ref, place_ref,
                out_ref, near_ref, far_ref, *, row_count, total_rows):
    row_start, _, stream_even = place_bits(place_ref)
    f = joined(next_ref, near_in_ref, far_in_ref, stream_even)
    planes, rows, depth = f[0].shape
    density, momenta, second = moments(f)
    markers = Markers(marker_ref, row_start, rows, total_rows, depth)
    total = None
    for start in markers.starts():
        _, _, selector, near, far = markers.weights(start)
        blocks = [force_ref[start + k] for k in range(markers.group)]
        values = blocks[0] if markers.group == 1 else jnp.concatenate(blocks, axis=1)
        added = spread_force([values[c : c + 1] for c in range(3)], selector, near, far)
        total = added if total is None else total + added
    forcing = forcing_fields(total, planes, rows, depth)
    out = collide(f, density, momenta, second, forcing, solid_ref[...] == 1.0)
    store_moved(out, out_ref, near_ref, far_ref, stream_even, row_count)


def join_kernel(next_ref, near_ref, far_ref, place_ref, out_ref):
    _, _, stream_even = place_bits(place_ref)
    for i, value in enumerate(joined(next_ref, near_ref, far_ref, stream_even)):
        out_ref[i] = value


def crossed(count, mask):
    return [(i, i ^ mask) for i in range(count)]


def paired(count, shift):
    swap = []
    for i in range(shift, count, 2):
        a, b = i % count, (i + 1) % count
        swap += [(a, b), (b, a)]
    return swap


def swapped(near, far, axis):
    count = lax.axis_size(axis)
    far = lax.ppermute(far, axis, paired(count, 1))
    near = lax.ppermute(near, axis, paired(count, 0))
    return near, far


def local(array):
    return pltpu.with_memory_space_constraint(array, pltpu.VMEM)


def call(kernel, inputs, outputs, place, scratch=(), in_hbm=False, out_hbm=False, **sizes):
    vmem = pl.BlockSpec(memory_space=pltpu.VMEM)
    smem = pl.BlockSpec(memory_space=pltpu.SMEM)
    anywhere = pl.BlockSpec(memory_space=pl.ANY)

    def body(*refs):
        kernel(*refs, **sizes)

    def result(shape):
        if out_hbm:
            return jax.ShapeDtypeStruct(shape, jnp.float32)
        return pltpu.VMEM(shape, jnp.float32)

    return pl.pallas_call(
        body,
        out_shape=tuple(result(s) for s in outputs),
        in_specs=[anywhere if in_hbm else vmem] * len(inputs) + [smem],
        out_specs=tuple(vmem for _ in outputs),
        scratch_shapes=list(scratch),
    )(*[a if in_hbm else local(a) for a in inputs], place)


def per_device(populations, solid, support, fractions, target, area):
    plane_count, row_count, depth_count = populations.shape[1:]
    own_markers = support.shape[0]
    groups = lax.axis_size("trans")
    total_rows = row_count * groups
    rows = row_count + 2 * HALO
    rank = lax.axis_index("trans")
    slab = lax.axis_index("stream")
    place = (rank * (4 * row_count) + (rank % 2) * 2 + slab % 2).astype(jnp.int32).reshape(1)
    side = len(forward_x)
    rim_shape = (20, plane_count, HALO, depth_count)
    f32 = jnp.float32

    packed, own, near, far = call(
        pack_kernel,
        [populations, solid, support[None], fractions, target, area[None]],
        [(8, own_markers), (20, plane_count, row_count, depth_count), rim_shape, rim_shape],
        place,
        scratch=[
            pltpu.VMEM(solid.shape, jnp.int32),
            pltpu.VMEM((1, own_markers), jnp.int32),
            pltpu.VMEM((3, own_markers), f32),
            pltpu.VMEM((3, own_markers), f32),
            pltpu.VMEM((1, own_markers), f32),
            pltpu.SemaphoreType.DMA((6,)),
        ],
        in_hbm=True,
    )
    near, far = swapped(near, far, "trans")
    markers = packed[None]
    mask = 1
    while mask < groups:
        arrived = lax.ppermute(markers, "trans", crossed(groups, mask))
        markers = jnp.concatenate([markers, arrived], axis=0)
        mask *= 2
    window_shape = (19, plane_count, rows, depth_count)
    side_shape = (side, rows, depth_count)
    following, near, far, solid_window = call(
        first_kernel,
        [own, near, far, markers],
        [window_shape, side_shape, side_shape, (plane_count, rows, depth_count)],
        place,
        scratch=[pltpu.VMEM((20, plane_count, rows, depth_count), f32)],
        total_rows=total_rows,
    )
    near, far = swapped(near, far, "stream")
    force, owned = call(
        force_kernel,
        [following, near, far, markers],
        [(groups, 3, own_markers)] * 2,
        place,
        row_count=row_count,
        total_rows=total_rows,
    )
    mask = groups // 2
    while mask:
        arrived = lax.ppermute(owned[mask : 2 * mask], "trans", crossed(groups, mask))
        owned = owned[:mask] + arrived
        mask //= 2
    own_force = owned[0]
    outgoing, near, far = call(
        last_kernel,
        [following, near, far, solid_window, markers, force],
        [(19, plane_count, row_count, depth_count)] + [(side, row_count, depth_count)] * 2,
        place,
        row_count=row_count,
        total_rows=total_rows,
    )
    near, far = swapped(near, far, "stream")
    (result,) = call(
        join_kernel,
        [outgoing, near, far],
        [(19, plane_count, row_count, depth_count)],
        place,
        out_hbm=True,
    )
    return (result, own_force)


def solution(mesh):
    placed = (
        P(None, "stream", "trans", None),
        P("stream", "trans", None),
        P(("stream", "trans")),
        P(None, ("stream", "trans")),
        P(None, ("stream", "trans")),
        P(("stream", "trans")),
    )

    return jax.shard_map(
        per_device,
        mesh=mesh,
        in_specs=placed,
        out_specs=(P(None, "stream", "trans", None), P(None, ("stream", "trans"))),
        check_vma=False,
    )
```

time: 45 us -> 40.2 us (0.89); the launches traced: 44.4 us -> 40 us
  waiting for transfers between devices: 13.3 us -> 20.3 us
  local copies, waits for them, and re-layouts: 5.6 us -> 0.01 us
  starting transfers between devices: 16.5 us -> 14.4 us
  Pallas kernels: 5.8 us -> 4 us
  other arithmetic: 2.36 us -> 0.6 us
    ppermute x6 -> x12, waiting for transfers between devices: 3.47 us -> 20.3 us  [the longest x3 9.37 us: per_device(): arrived = lax.ppermute(owned[mask:2 * mask], 'trans', crossed(groups, mask))]
    all_to_all x2 -> x0, waiting for transfers between devices: 9.88 us -> none  [the longest x1 6.62 us: per_device(): markers = lax.all_to_all(copies, 'trans', 0, 0, tiled=False)]
    all_to_all x2 -> x0, starting transfers between devices: 6.81 us -> none  [the longest x1 3.47 us: per_device(): lax.all_to_all(force, 'trans', 0, 0, tiled=False)]
    ppermute x6 -> x12, starting transfers between devices: 9.69 us -> 14.4 us  [the longest x3 8.17 us: per_device(): arrived = lax.ppermute(markers, 'trans', crossed(groups, mask))]
    unnamed x24 -> x0, local copies, waits for them, and re-layouts: 3.38 us -> none
    pallas_call x2 -> x5, Pallas kernels: 5.8 us -> 4 us  [call(): pl.pallas_call(body, out_shape=tuple((result(s) for s in outputs)), in_sp...]
    another operation x2 -> x0, local copies, waits for them, and re-layouts: 1.59 us -> none  [the longest x1 0.83 us: per_device(): planes.append(jnp.stack([outgoing[i, 0], from_high[backward_x.index(i)]]))]
    concatenate x2 -> x3, other arithmetic: 1.03 us -> 0.01 us  [per_device(): markers = jnp.concatenate([markers, arrived], axis=0)]
  transfers between devices with their start and end apart: 8 -> 12, of which waited for: 5 -> 8; matrix products, arithmetic and copies ran while one was open for 8% -> 1% of each run, Pallas kernels for 0% -> 2%
where the time goes in v2:
time: 40.2 us; the launch traced here: 40 us
  waiting for transfers between devices  20.3 us (50%)
  starting transfers between devices  14.4 us (36%)
  Pallas kernels  4 us (10%)
  between operations  0.72 us (2%)
  other arithmetic  0.6 us (1%)
    ppermute x3, waiting for transfers between devices, per_device(): arrived = lax.ppermute(owned[mask:2 * mask], 'trans', crossed(groups, mask))  9.37 us
    ppermute x3, starting transfers between devices, per_device(): arrived = lax.ppermute(markers, 'trans', crossed(groups, mask))  8.17 us
    ppermute x3, waiting for transfers between devices, swapped(): far = lax.ppermute(far, axis, paired(count, 1))  5.18 us
    ppermute x3, starting transfers between devices, swapped(): far = lax.ppermute(far, axis, paired(count, 1))  4.56 us
    pallas_call x5, Pallas kernels, call(): pl.pallas_call(body, out_shape=tuple((result(s) for s in outputs)), in_sp...  4 us
    ppermute x3, waiting for transfers between devices, per_device(): arrived = lax.ppermute(markers, 'trans', crossed(groups, mask))  3.22 us
    ppermute x3, waiting for transfers between devices, swapped(): near = lax.ppermute(near, axis, paired(count, 0))  2.51 us
    ppermute x3, starting transfers between devices, swapped(): near = lax.ppermute(near, axis, paired(count, 0))  1.63 us
  transfers between devices with their start and end apart: 12, of which 8 were waited for; matrix products, arithmetic and copies ran while one was open for 1% of the time, Pallas kernels for 2%

profile of v2, /device:TPU:0, one launch (start us, length us, event | category | flops | bytes accessed | tf_op | source)
XLA Modules:
  0.0 40.0 jit_solution(10392940747429759379)
XLA Ops:
  0.7 1.1 %shard_map.77 = (f32[8,128]{1,0:T(8,128)S(1)}, f32[20,2,8,128]{3,2,1,0:T(8,128)S(1)}, f32[20,2,4,128]{3,2,1,0:T(4,128)S(1)}, f32[20,2,4,128]{3,2,1,0:T(4,128)S(1)}) custom-call(f32[19,2,8,128]{3,2,1,0:T(8,128)} %refs_0_.1, s32[2,8,128]{2,1,0:T(8,128)} %refs_1_.1, s32[1,128]{1,0:T(1,128)} %bitcast.10, f32[3,128]{1,0:T(4,128)} %refs_3_.1, f32[3,128]{1,0:T(4,128)} %refs_4_.1, ...), custom_call_target="tpu_custom_call" | custom-call | tf_op jit(solution)/shard_map/pallas_call | solution.py:405
  1.7 3.0 %collective-permute-start.2 = (f32[1,8,128]{2,1,0:T(8,128)S(1)}, f32[1,8,128]{2,1,0:T(8,128)S(1)}, u32[]{:S(2)}, u32[]{:S(2)}) collective-permute-start(f32[1,8,128]{2,1,0:T(8,128)S(1)} %bitcast.6), channel_id=1, source_target_pairs={{0,1},{1,0},{2,3},{3,2},{4,5},{5,4},{6,7},{7,6},{8,9},{9,8},{10,11... | collective-permute-start | bytes 12296 | tf_op jit(solution)/shard_map/ppermute | solution.py:446
  4.8 1.6 %collective-permute-done.2 = f32[1,8,128]{2,1,0:T(8,128)S(1)} collective-permute-done((f32[1,8,128]{2,1,0:T(8,128)S(1)}, f32[1,8,128]{2,1,0:T(8,128)S(1)}, u32[]{:S(2)}, u32[]{:S(2)}) %collective-permute-start.2) | collective-permute-done | bytes 4128 | tf_op jit(solution)/shard_map/ppermute | solution.py:446
  6.4 2.1 %collective-permute-start.3 = (f32[2,8,128]{2,1,0:T(8,128)S(1)}, f32[2,8,128]{2,1,0:T(8,128)S(1)}, u32[]{:S(2)}, u32[]{:S(2)}) collective-permute-start(f32[2,8,128]{2,1,0:T(8,128)S(1)} %pad_maximum_fusion.2), channel_id=1, source_target_pairs={{0,2},{1,3},{2,0},{3,1},{4,6},{5,7},{6,4},{7,5},{8,10},{9,11},{10,... | collective-permute-start | bytes 24584 | tf_op jit(solution)/shard_map/ppermute | solution.py:446
  8.5 1.6 %collective-permute-done.3 = f32[2,8,128]{2,1,0:T(8,128)S(1)} collective-permute-done((f32[2,8,128]{2,1,0:T(8,128)S(1)}, f32[2,8,128]{2,1,0:T(8,128)S(1)}, u32[]{:S(2)}, u32[]{:S(2)}) %collective-permute-start.3) | collective-permute-done | bytes 8224 | tf_op jit(solution)/shard_map/ppermute | solution.py:446
  10.1 3.0 %collective-permute-start.4 = (f32[4,8,128]{2,1,0:T(8,128)S(1)}, f32[4,8,128]{2,1,0:T(8,128)S(1)}, u32[]{:S(2)}, u32[]{:S(2)}) collective-permute-start(f32[4,8,128]{2,1,0:T(8,128)S(1)} %pad_maximum_fusion.1), channel_id=1, source_target_pairs={{0,4},{1,5},{2,6},{3,7},{4,0},{5,1},{6,2},{7,3},{8,12},{9,13},{10,... | collective-permute-start | bytes 49160 | tf_op jit(solution)/shard_map/ppermute | solution.py:446
  13.1 1.5 %collective-permute-start = (f32[20,2,4,128]{3,2,1,0:T(4,128)S(1)}, f32[20,2,4,128]{3,2,1,0:T(4,128)S(1)}, u32[]{:S(2)}, u32[]{:S(2)}) collective-permute-start(f32[20,2,4,128]{3,2,1,0:T(4,128)S(1)} %get-tuple-element.16), channel_id=1, source_target_pairs={{0,1},{1,0},{2,3},{3,2},{4,5},{5,4},{6,7},{7,6},{8,9},{9,8},{10,11... | collective-permute-start | bytes 245768 | tf_op jit(solution)/shard_map/ppermute | solution.py:384
  14.6 1.3 %collective-permute-start.1 = (f32[20,2,4,128]{3,2,1,0:T(4,128)S(1)}, f32[20,2,4,128]{3,2,1,0:T(4,128)S(1)}, u32[]{:S(2)}, u32[]{:S(2)}) collective-permute-start(f32[20,2,4,128]{3,2,1,0:T(4,128)S(1)} %get-tuple-element.17), channel_id=1, source_target_pairs={{1,2},{2,1},{3,4},{4,3},{5,6},{6,5},{7,0},{0,7},{9,10},{10,9},{11,... | collective-permute-start | bytes 245768 | tf_op jit(solution)/shard_map/ppermute | solution.py:383
  15.9 0.0 collective-permute-done.4
  16.0 2.5 %collective-permute-done.refs_1_ = f32[20,2,4,128]{3,2,1,0:T(4,128)S(1)} collective-permute-done((f32[20,2,4,128]{3,2,1,0:T(4,128)S(1)}, f32[20,2,4,128]{3,2,1,0:T(4,128)S(1)}, u32[]{:S(2)}, u32[]{:S(2)}) %collective-permute-start) | collective-permute-done | bytes 81952 | tf_op jit(solution)/shard_map/ppermute | solution.py:384
  18.5 3.3 %collective-permute-done.1.refs_2_ = f32[20,2,4,128]{3,2,1,0:T(4,128)S(1)} collective-permute-done((f32[20,2,4,128]{3,2,1,0:T(4,128)S(1)}, f32[20,2,4,128]{3,2,1,0:T(4,128)S(1)}, u32[]{:S(2)}, u32[]{:S(2)}) %collective-permute-start.1) | collective-permute-done | bytes 81952 | tf_op jit(solution)/shard_map/ppermute | solution.py:383
  21.8 1.2 %shard_map.78 = (f32[19,2,16,128]{3,2,1,0:T(8,128)S(1)}, f32[5,16,128]{2,1,0:T(8,128)S(1)}, f32[5,16,128]{2,1,0:T(8,128)S(1)}, f32[2,16,128]{2,1,0:T(8,128)S(1)}) custom-call(f32[20,2,8,128]{3,2,1,0:T(8,128)S(1)} %get-tuple-element.15.refs_0_, f32[20,2,4,128]{3,2,1,0:T(4,128)S(1)} %collective-permute-done.refs_1_, ...), custom_call_target="tpu_custom_call" | custom-call | tf_op jit(solution)/shard_map/pallas_call | solution.py:405
  23.0 0.1 collective-permute-start.5
  23.0 1.6 %collective-permute-start.6 = (f32[5,16,128]{2,1,0:T(8,128)S(1)}, f32[5,16,128]{2,1,0:T(8,128)S(1)}, u32[]{:S(2)}, u32[]{:S(2)}) collective-permute-start(f32[5,16,128]{2,1,0:T(8,128)S(1)} %get-tuple-element.21), channel_id=1, source_target_pairs={{8,16},{16,8},{24,0},{0,24},{9,17},{17,9},{25,1},{1,25},{10,18},{1... | collective-permute-start | bytes 122888 | tf_op jit(solution)/shard_map/ppermute | solution.py:383
  24.7 0.0 collective-permute-done.5.refs_1_
  24.7 1.9 %collective-permute-done.6.refs_2_ = f32[5,16,128]{2,1,0:T(8,128)S(1)} collective-permute-done((f32[5,16,128]{2,1,0:T(8,128)S(1)}, f32[5,16,128]{2,1,0:T(8,128)S(1)}, u32[]{:S(2)}, u32[]{:S(2)}) %collective-permute-start.6) | collective-permute-done | bytes 40992 | tf_op jit(solution)/shard_map/ppermute | solution.py:383
  26.5 0.4 shard_map.79
  27.0 0.1 collective-permute-start.9
  27.0 4.5 %collective-permute-done.9 = f32[4,3,128]{2,1,0:T(4,128)S(1)} collective-permute-done((f32[4,3,128]{2,1,0:T(4,128)S(1)}, f32[4,3,128]{2,1,0:T(4,128)S(1)}, u32[]{:S(2)}, u32[]{:S(2)}) %collective-permute-start.9) | collective-permute-done | bytes 6176 | tf_op jit(solution)/shard_map/ppermute | solution.py:470
  31.6 0.0 collective-permute-start.10
  31.6 3.6 %collective-permute-done.10 = f32[2,3,128]{2,1,0:T(4,128)S(1)} collective-permute-done((f32[2,3,128]{2,1,0:T(4,128)S(1)}, f32[2,3,128]{2,1,0:T(4,128)S(1)}, u32[]{:S(2)}, u32[]{:S(2)}) %collective-permute-start.10) | collective-permute-done | bytes 3104 | tf_op jit(solution)/shard_map/ppermute | solution.py:470
  35.2 0.0 collective-permute-start.11
  35.2 0.7 %shard_map.80 = (f32[19,2,8,128]{3,2,1,0:T(8,128)S(1)}, f32[5,8,128]{2,1,0:T(8,128)S(1)}, f32[5,8,128]{2,1,0:T(8,128)S(1)}) custom-call(f32[19,2,16,128]{3,2,1,0:T(8,128)S(1)} %get-tuple-element.19.refs_0_, f32[5,16,128]{2,1,0:T(8,128)S(1)} %collective-permute-done.5.refs_1_, f32[5,16,128]{2,1,0:T(8,128)S(1)} %collective-permute-done.6.refs_2_, ...), custom_call_target="tpu_custom_call" | custom-call | tf_op jit(solution)/shard_map/pallas_call | solution.py:405
  35.9 0.1 collective-permute-start.7
  35.9 1.6 %collective-permute-start.8 = (f32[5,8,128]{2,1,0:T(8,128)S(1)}, f32[5,8,128]{2,1,0:T(8,128)S(1)}, u32[]{:S(2)}, u32[]{:S(2)}) collective-permute-start(f32[5,8,128]{2,1,0:T(8,128)S(1)} %get-tuple-element.26), channel_id=1, source_target_pairs={{8,16},{16,8},{24,0},{0,24},{9,17},{17,9},{25,1},{1,25},{10,18},{1... | collective-permute-start | bytes 61448 | tf_op jit(solution)/shard_map/ppermute | solution.py:383
  37.6 1.2 %collective-permute-done.11 = f32[1,3,128]{2,1,0:T(4,128)S(1)} collective-permute-done((f32[1,3,128]{2,1,0:T(4,128)S(1)}, f32[1,3,128]{2,1,0:T(4,128)S(1)}, u32[]{:S(2)}, u32[]{:S(2)}) %collective-permute-start.11) | collective-permute-done | bytes 1568 | tf_op jit(solution)/shard_map/ppermute | solution.py:470
  38.8 0.6 %fusion = f32[3,128]{1,0:T(4,128)} fusion(f32[1,3,128]{2,1,0:T(4,128)S(1)} %collective-permute-done.11, f32[2,3,128]{2,1,0:T(4,128)S(1)} %slice_add_fusion.1), kind=kLoop, calls=%fused_computation.6 | loop fusion | flops 384 | bytes 4608 | tf_op jit(solution)/shard_map/squeeze | solution.py:473
  39.4 0.0 collective-permute-done.7.refs_1_
  39.4 0.0 collective-permute-done.8.refs_2_
  39.4 0.7 %shard_map.81 = f32[19,2,8,128]{3,2,1,0:T(8,128)} custom-call(f32[19,2,8,128]{3,2,1,0:T(8,128)S(1)} %get-tuple-element.24.refs_0_, f32[5,8,128]{2,1,0:T(8,128)S(1)} %collective-permute-done.7.refs_1_, f32[5,8,128]{2,1,0:T(8,128)S(1)} %collective-permute-done.8.refs_2_, s32[1]{0:T(128)} %bitcast.2.refs_6_.refs_4_.refs_3_), custom_call_target="tpu_custom_call" | custom-call | tf_op jit(solution)/shard_map/pallas_call | solution.py:405
  (8 shorter events, 0.0 us)
Async XLA Ops:
  1.7 4.6 %collective-permute-start.2 = (f32[1,8,128]{2,1,0:T(8,128)S(1)}, f32[1,8,128]{2,1,0:T(8,128)S(1)}, u32[]{:S(2)}, u32[]{:S(2)}) collective-permute-start(f32[1,8,128]{2,1,0:T(8,128)S(1)} %bitcast.6), channel_id=1, source_target_pairs={{0,1},{1,0},{2,3},{3,2},{4,5},{5,4},{6,7},{7,6},{8,9},{9,8},{10,11... | collective-permute-start | bytes 12296 | tf_op jit(solution)/shard_map/ppermute | solution.py:446
  6.4 3.7 %collective-permute-start.3 = (f32[2,8,128]{2,1,0:T(8,128)S(1)}, f32[2,8,128]{2,1,0:T(8,128)S(1)}, u32[]{:S(2)}, u32[]{:S(2)}) collective-permute-start(f32[2,8,128]{2,1,0:T(8,128)S(1)} %pad_maximum_fusion.2), channel_id=1, source_target_pairs={{0,2},{1,3},{2,0},{3,1},{4,6},{5,7},{6,4},{7,5},{8,10},{9,11},{10,... | collective-permute-start | bytes 24584 | tf_op jit(solution)/shard_map/ppermute | solution.py:446
  10.1 5.8 %collective-permute-start.4 = (f32[4,8,128]{2,1,0:T(8,128)S(1)}, f32[4,8,128]{2,1,0:T(8,128)S(1)}, u32[]{:S(2)}, u32[]{:S(2)}) collective-permute-start(f32[4,8,128]{2,1,0:T(8,128)S(1)} %pad_maximum_fusion.1), channel_id=1, source_target_pairs={{0,4},{1,5},{2,6},{3,7},{4,0},{5,1},{6,2},{7,3},{8,12},{9,13},{10,... | collective-permute-start | bytes 49160 | tf_op jit(solution)/shard_map/ppermute | solution.py:446
  13.1 5.3 %collective-permute-start = (f32[20,2,4,128]{3,2,1,0:T(4,128)S(1)}, f32[20,2,4,128]{3,2,1,0:T(4,128)S(1)}, u32[]{:S(2)}, u32[]{:S(2)}) collective-permute-start(f32[20,2,4,128]{3,2,1,0:T(4,128)S(1)} %get-tuple-element.16), channel_id=1, source_target_pairs={{0,1},{1,0},{2,3},{3,2},{4,5},{5,4},{6,7},{7,6},{8,9},{9,8},{10,11... | collective-permute-start | bytes 245768 | tf_op jit(solution)/shard_map/ppermute | solution.py:384
  14.6 7.1 %collective-permute-start.1 = (f32[20,2,4,128]{3,2,1,0:T(4,128)S(1)}, f32[20,2,4,128]{3,2,1,0:T(4,128)S(1)}, u32[]{:S(2)}, u32[]{:S(2)}) collective-permute-start(f32[20,2,4,128]{3,2,1,0:T(4,128)S(1)} %get-tuple-element.17), channel_id=1, source_target_pairs={{1,2},{2,1},{3,4},{4,3},{5,6},{6,5},{7,0},{0,7},{9,10},{10,9},{11,... | collective-permute-start | bytes 245768 | tf_op jit(solution)/shard_map/ppermute | solution.py:383
  23.0 1.7 %collective-permute-start.5 = (f32[5,16,128]{2,1,0:T(8,128)S(1)}, f32[5,16,128]{2,1,0:T(8,128)S(1)}, u32[]{:S(2)}, u32[]{:S(2)}) collective-permute-start(f32[5,16,128]{2,1,0:T(8,128)S(1)} %get-tuple-element.20), channel_id=1, source_target_pairs={{0,8},{8,0},{16,24},{24,16},{1,9},{9,1},{17,25},{25,17},{2,10},{10... | collective-permute-start | bytes 122888 | tf_op jit(solution)/shard_map/ppermute | solution.py:384
  23.0 3.5 %collective-permute-start.6 = (f32[5,16,128]{2,1,0:T(8,128)S(1)}, f32[5,16,128]{2,1,0:T(8,128)S(1)}, u32[]{:S(2)}, u32[]{:S(2)}) collective-permute-start(f32[5,16,128]{2,1,0:T(8,128)S(1)} %get-tuple-element.21), channel_id=1, source_target_pairs={{8,16},{16,8},{24,0},{0,24},{9,17},{17,9},{25,1},{1,25},{10,18},{1... | collective-permute-start | bytes 122888 | tf_op jit(solution)/shard_map/ppermute | solution.py:383
  27.0 4.6 %collective-permute-start.9 = (f32[4,3,128]{2,1,0:T(4,128)S(1)}, f32[4,3,128]{2,1,0:T(4,128)S(1)}, u32[]{:S(2)}, u32[]{:S(2)}) collective-permute-start(f32[4,3,128]{2,1,0:T(4,128)S(1)} %slice.19), channel_id=1, source_target_pairs={{0,4},{1,5},{2,6},{3,7},{4,0},{5,1},{6,2},{7,3},{8,12},{9,13},{10,... | collective-permute-start | bytes 18440 | tf_op jit(solution)/shard_map/ppermute | solution.py:470
  31.6 3.6 %collective-permute-start.10 = (f32[2,3,128]{2,1,0:T(4,128)S(1)}, f32[2,3,128]{2,1,0:T(4,128)S(1)}, u32[]{:S(2)}, u32[]{:S(2)}) collective-permute-start(f32[2,3,128]{2,1,0:T(4,128)S(1)} %slice.25), channel_id=1, source_target_pairs={{0,2},{1,3},{2,0},{3,1},{4,6},{5,7},{6,4},{7,5},{8,10},{9,11},{10,... | collective-permute-start | bytes 9224 | tf_op jit(solution)/shard_map/ppermute | solution.py:470
  35.2 3.6 %collective-permute-start.11 = (f32[1,3,128]{2,1,0:T(4,128)S(1)}, f32[1,3,128]{2,1,0:T(4,128)S(1)}, u32[]{:S(2)}, u32[]{:S(2)}) collective-permute-start(f32[1,3,128]{2,1,0:T(4,128)S(1)} %slice.27), channel_id=1, source_target_pairs={{0,1},{1,0},{2,3},{3,2},{4,5},{5,4},{6,7},{7,6},{8,9},{9,8},{10,11... | collective-permute-start | bytes 4616 | tf_op jit(solution)/shard_map/ppermute | solution.py:470
  35.9 3.5 %collective-permute-start.7 = (f32[5,8,128]{2,1,0:T(8,128)S(1)}, f32[5,8,128]{2,1,0:T(8,128)S(1)}, u32[]{:S(2)}, u32[]{:S(2)}) collective-permute-start(f32[5,8,128]{2,1,0:T(8,128)S(1)} %get-tuple-element.25), channel_id=1, source_target_pairs={{0,8},{8,0},{16,24},{24,16},{1,9},{9,1},{17,25},{25,17},{2,10},{10... | collective-permute-start | bytes 61448 | tf_op jit(solution)/shard_map/ppermute | solution.py:384
  35.9 3.4 %collective-permute-start.8 = (f32[5,8,128]{2,1,0:T(8,128)S(1)}, f32[5,8,128]{2,1,0:T(8,128)S(1)}, u32[]{:S(2)}, u32[]{:S(2)}) collective-permute-start(f32[5,8,128]{2,1,0:T(8,128)S(1)} %get-tuple-element.26), channel_id=1, source_target_pairs={{8,16},{16,8},{24,0},{0,24},{9,17},{17,9},{25,1},{1,25},{10,18},{1... | collective-permute-start | bytes 61448 | tf_op jit(solution)/shard_map/ppermute | solution.py:383
